TPU v7x, 32 devices: a whole 2x2x4 slice. The times are simulated.
32 devices in a mesh: grp: 2 (over y), wide: 8 (over z, x), narrow: 2 (over core).
Axes of the slice: x: 2, y: 2, z: 4, core: 2. Of those that a mesh axis runs over, the one named last changes fastest.
Arguments:
- node_latent: bfloat16 [5120, 512], P(('grp', 'wide', 'narrow')), parts along dimension 0, may hold values from -6 to 6
- fine_edges: bfloat16 [30720, 512], P(('grp', 'wide', 'narrow')), parts along dimension 0, may hold values from -6 to 6
- fine_senders: int32 [30720], P(('grp', 'wide', 'narrow')), parts along dimension 0, may hold values from 0 to 2559, as said below
- fine_receivers: int32 [30720], P(('grp', 'wide', 'narrow')), parts along dimension 0, may hold values from 0 to 2559, as said below
- coarse_edges: bfloat16 [1024, 512], P(('grp', 'wide', 'narrow')), parts along dimension 0, may hold values from -6 to 6
- coarse_senders: int32 [1024], P(('grp', 'wide', 'narrow')), parts along dimension 0, may hold values from 0 to 2403, as said below
- coarse_receivers: int32 [1024], P(('grp', 'wide', 'narrow')), parts along dimension 0, may hold values from 0 to 2403, as said below
- edge_weight_in: bfloat16 [1536, 512], replicated, may hold values from -0.15625 to 0.15625
- edge_bias: float32 [512], replicated, may hold values from -3 to 3
- edge_weight_out: bfloat16 [512, 512], replicated, may hold values from -0.25 to 0.25
- edge_gain: float32 [512], replicated, may hold values from 0.5 to 1.5
- edge_shift: float32 [512], replicated, may hold values from -2 to 2
- node_weight_in: bfloat16 [1024, 512], replicated, may hold values from -0.1875 to 0.1875
- node_bias: float32 [512], replicated, may hold values from -3 to 3
- node_weight_out: bfloat16 [512, 512], replicated, may hold values from -0.25 to 0.25
- node_gain: float32 [512], replicated, may hold values from 0.5 to 1.5
- node_shift: float32 [512], replicated, may hold values from -2 to 2
Outputs:
- node_out: bfloat16 [5120, 512], P(('grp', 'wide', 'narrow')), parts along dimension 0
There are 2 independent parts, one for each index of `grp`. A program takes and returns all parts, laid end to end along the dimension named above; an argument that names none is the same for every part. Nothing has to cross between parts.
Inputs may be any that keep to these rules, and one draw needn't show every extreme that they name: `fine_receivers`: node v belongs to device v // 160 (devices numbered wide index times 2 plus narrow index) and to patch v // 320. Each block of 960 fine edges belongs to one device, in order, and its receivers are that device's nodes. `fine_senders`: the sender of a fine edge lies in the receiver's patch p, or is a boundary node (v % 160 >= 140) of a device of patch p - 1 or p + 1, modulo 8. `coarse_receivers`: coarse nodes are the nodes v with v % 160 < 4. Each block of 32 coarse edges belongs to one device, in order, and its receivers are that device's coarse nodes; each coarse node receives at least one. `coarse_senders`: every coarse sender is a coarse node, on any device.
All inputs are finite; a program needn't handle non-finite values.
Results may differ from a plain program's by a relative error of at most 0.0053.
Values may be sent and summed in bfloat16 or wider, within the bound.
No kernel may reach another device: no remote copies, remote signals or barrier semaphores. Data moves between devices by JAX's collectives and lax.ppermute only.
A program may use at most 64 MiB of HBM per device.

v0:
```python
import jax
import jax.numpy as jnp
from jax import lax
from jax.sharding import PartitionSpec as P

COARSE_DEV = 4


def with_halo(shard, sides, width):
    for axis, dim in sides:
        devices, length = (lax.axis_size(axis), shard.shape[dim])
        up = [(i, (i + 1) % devices) for i in range(devices)]
        down = [(j, i) for i, j in up]
        last = lax.slice_in_dim(shard, length - width, length, axis=dim)
        first = lax.slice_in_dim(shard, 0, width, axis=dim)
        before = lax.ppermute(last, axis, up)
        after = lax.ppermute(first, axis, down)
        shard = jnp.concatenate([before, shard, after], axis=dim)
    return shard


def layer_norm(values, gain_vector, shift_vector):
    center = values - jnp.mean(values, axis=-1, keepdims=True)
    spread = jnp.mean(center * center, axis=-1, keepdims=True)
    return center * lax.rsqrt(spread + 1e-05) * gain_vector + shift_vector


def run_mlp(preact, weight_out, gain_vector, shift_vector):
    hidden = jax.nn.silu(preact).astype(jnp.bfloat16)
    output = jnp.dot(hidden, weight_out, preferred_element_type=jnp.float32)
    return layer_norm(output, gain_vector, shift_vector)


def shards(
    node_latent,
    fine_edges,
    fine_senders,
    fine_receivers,
    coarse_edges,
    coarse_senders,
    coarse_receivers,
    edge_weight_in,
    edge_bias,
    edge_weight_out,
    edge_gain,
    edge_shift,
    node_weight_in,
    node_bias,
    node_weight_out,
    node_gain,
    node_shift,
):
    node_count, latent_width = node_latent.shape
    halo_count = node_count // 8
    halo_first = node_count - halo_count
    n_narrow = lax.axis_size("narrow")
    wide_index = lax.axis_index("wide")
    narrow_index = lax.axis_index("narrow")
    device = wide_index * n_narrow + narrow_index
    patch_size = node_count * n_narrow
    patch_start = wide_index * patch_size
    w_edge = edge_weight_in[:latent_width]
    w_send = edge_weight_in[latent_width : 2 * latent_width]
    w_recv = edge_weight_in[2 * latent_width :]
    patch_rows = lax.all_gather(node_latent, "narrow", axis=0, tiled=True)
    edge_rows = patch_rows.reshape(n_narrow, node_count, latent_width)[:, halo_first:].reshape(
        -1, latent_width
    )
    halves = jnp.arange(n_narrow * halo_count, dtype=jnp.int32) // halo_count
    within_halo = jnp.arange(n_narrow * halo_count, dtype=jnp.int32) % halo_count
    edge_ids = patch_start + halves * node_count + halo_first + within_halo
    rows_near, ids_near = (
        with_halo(edge_rows[None], (("wide", 0),), 1),
        with_halo(edge_ids[None], (("wide", 0),), 1),
    )
    remote_rows = jnp.concatenate([rows_near[0], rows_near[2]], axis=0)
    remote_ids = jnp.concatenate([ids_near[0], ids_near[2]], axis=0)
    node_proj = jnp.dot(node_latent, w_recv, preferred_element_type=jnp.float32)
    patch_proj = jnp.dot(patch_rows, w_send, preferred_element_type=jnp.float32)
    remote_proj = jnp.dot(remote_rows, w_send, preferred_element_type=jnp.float32)
    offsets = fine_senders - patch_start
    inside = (offsets >= 0) & (offsets < patch_size)
    inner_pos = jnp.clip(offsets, 0, patch_size - 1)
    matches = fine_senders[:, None] == remote_ids[None, :]
    positions = jnp.arange(remote_ids.shape[0], dtype=jnp.int32)
    outer_pos = jnp.sum(jnp.where(matches, positions[None, :], 0), axis=1)
    sender_term = jnp.where(inside[:, None], patch_proj[inner_pos], remote_proj[outer_pos])
    local_recv = fine_receivers - device * node_count
    fine_pre = (
        jnp.dot(fine_edges, w_edge, preferred_element_type=jnp.float32)
        + sender_term
        + node_proj[local_recv]
    )
    table_slots = coarse_senders // node_count * COARSE_DEV + coarse_senders % node_count
    shard_rows = lax.all_gather(node_latent[:COARSE_DEV], ("wide", "narrow"), axis=0, tiled=True)
    wanted = jnp.arange(shard_rows.shape[0], dtype=jnp.int32)
    selector = (table_slots[:, None] == wanted[None, :]).astype(jnp.bfloat16)
    coarse_rows = jnp.dot(selector, shard_rows, preferred_element_type=jnp.float32).astype(
        jnp.bfloat16
    )
    coarse_local = coarse_receivers - device * node_count
    coarse_pre = jnp.dot(coarse_edges, w_edge, preferred_element_type=jnp.float32)
    coarse_pre = (
        coarse_pre
        + jnp.dot(coarse_rows, w_send, preferred_element_type=jnp.float32)
        + node_proj[coarse_local]
    )
    preact = jnp.concatenate([fine_pre, coarse_pre], axis=0) + edge_bias
    messages = run_mlp(preact, edge_weight_out, edge_gain, edge_shift).astype(jnp.bfloat16)
    receivers_all = jnp.concatenate([local_recv, coarse_local], axis=0)
    node_slots = jnp.arange(node_count, dtype=jnp.int32)
    incidence = (node_slots[:, None] == receivers_all[None, :]).astype(jnp.bfloat16)
    summed = jnp.dot(incidence, messages, preferred_element_type=jnp.float32).astype(jnp.bfloat16)
    node_pre = jnp.dot(
        node_latent, node_weight_in[:latent_width], preferred_element_type=jnp.float32
    )
    node_pre = node_pre + jnp.dot(
        summed, node_weight_in[latent_width:], preferred_element_type=jnp.float32
    )
    node_pre = node_pre + node_bias
    node_update = run_mlp(node_pre, node_weight_out, node_gain, node_shift)
    return (node_latent.astype(jnp.float32) + node_update).astype(jnp.bfloat16)


def solution(mesh):
    return jax.shard_map(
        shards,
        mesh=mesh,
        in_specs=(
            P(("grp", "wide", "narrow"), None),
            P(("grp", "wide", "narrow"), None),
            P(("grp", "wide", "narrow")),
            P(("grp", "wide", "narrow")),
            P(("grp", "wide", "narrow"), None),
            P(("grp", "wide", "narrow")),
            P(("grp", "wide", "narrow")),
            P(),
            P(),
            P(),
            P(),
            P(),
            P(),
            P(),
            P(),
            P(),
            P(),
        ),
        out_specs=P(("grp", "wide", "narrow"), None),
        check_vma=False,
    )
```

profile of v0, /device:TPU:0, one launch (start us, length us, event | category | flops | bytes accessed | tf_op | source)
XLA Modules:
  0.0 80.6 jit_solution(10833074330517770571)
XLA Ops:
  0.6 3.0 %collective-permute-start.2 = (s32[1,40]{1,0:T(1,128)}, s32[1,40]{1,0:T(1,128)}, u32[]{:S(2)}, u32[]{:S(2)}) collective-permute-start(s32[1,40]{1,0:T(1,128)} %fusion.32), channel_id=1, source_target_pairs={{0,2},{2,4},{4,6},{6,8},{8,10},{10,12},{12,14},{14,0},{1,3},{3,5},... | collective-permute-start | bytes 488 | tf_op jit(solution)/shard_map/ppermute | solution.py:16
  3.5 3.0 %collective-permute-start.3 = (s32[1,40]{1,0:T(1,128)}, s32[1,40]{1,0:T(1,128)}, u32[]{:S(2)}, u32[]{:S(2)}) collective-permute-start(s32[1,40]{1,0:T(1,128)} %fusion.32), channel_id=1, source_target_pairs={{2,0},{4,2},{6,4},{8,6},{10,8},{12,10},{14,12},{0,14},{3,1},{5,3},... | collective-permute-start | bytes 488 | tf_op jit(solution)/shard_map/ppermute | solution.py:17
  6.6 2.2 %all_gather.6 = bf16[320,512]{1,0:T(8,128)(2,1)S(1)} all-gather(bf16[160,512]{1,0:T(8,128)(2,1)} %param.17), channel_id=1, replica_groups=mesh['grp'=2,'wide'=8,'narrow'=2] {'narrow'}, dimensions={0}, use_global_device_ids=true | all-gather | bytes 491520 | tf_op jit(solution)/shard_map/all_gather | solution.py:65
  10.2 4.7 %collective-permute-start.1 = (bf16[1,40,512]{2,1,0:T(8,128)(2,1)}, bf16[1,40,512]{2,1,0:T(8,128)(2,1)}, u32[]{:S(2)}, u32[]{:S(2)}) collective-permute-start(bf16[1,40,512]{2,1,0:T(8,128)(2,1)} %broadcast_in_dim_reshape.3), channel_id=1, source_target_pairs={{2,0},{4,2},{6,4},{8,6},{10,8},{12,10},{14,12},{0,14},{3,1},{5,3},... | collective-permute-start | bytes 122888 | tf_op jit(solution)/shard_map/ppermute | solution.py:17
  14.9 1.4 %fusion.10 = f32[160,512]{1,0:T(8,128)S(1)} fusion(bf16[160,512]{1,0:T(8,128)(2,1)} %param.17, bf16[1536,512]{1,0:T(8,128)(2,1)} %param.24), kind=kOutput, calls=%fused_computation.21 | convolution fusion | flops 83886080 | bytes 1015808 | tf_op jit(solution)/shard_map/dot_general | solution.py:78
  16.3 1.3 %fusion.21 = f32[320,512]{1,0:T(8,128)S(1)} fusion(bf16[320,512]{1,0:T(8,128)(2,1)} %copy-done.4, bf16[1536,512]{1,0:T(8,128)(2,1)S(1)} %copy-done.2), kind=kOutput, calls=%fused_computation.32 | convolution fusion | flops 167772160 | bytes 1507328 | tf_op jit(solution)/shard_map/dot_general | solution.py:79
  18.8 1.3 %slice_bitcast_fusion = bf16[1,4,512]{2,1,0:T(4,128)(2,1)} fusion(bf16[160,512]{1,0:T(8,128)(2,1)} %param.17), kind=kLoop, calls=%fused_computation.53 | loop fusion | bytes 8192
  20.8 2.0 %fusion.16 = f32[960,512]{1,0:T(8,128)} fusion(bf16[960,512]{1,0:T(8,128)(2,1)S(1)} %copy-done, bf16[1536,512]{1,0:T(8,128)(2,1)S(1)} %copy-done.2), kind=kOutput, calls=%fused_computation.27 | convolution fusion | flops 503316480 | bytes 3473408 | tf_op jit(solution)/shard_map/dot_general | solution.py:90
  22.7 1.2 %compare_select_fusion.3 = (s32[32]{0:T(128)S(1)}, s32[32]{0:T(128)}) fusion(s32[32]{0:T(128)} %param.23, s32[]{:T(128)S(6)} %mul.76), kind=kLoop, calls=%fused_computation.55 | loop fusion | flops 128 | bytes 388 | tf_op jit(solution)/shard_map/select_n | solution.py:106
  24.5 18.7 %all-gather = bf16[16,4,512]{2,1,0:T(4,128)(2,1)} all-gather(bf16[1,4,512]{2,1,0:T(4,128)(2,1)S(1)} %copy-done.8), channel_id=1, replica_groups=mesh['grp'=2,'wide'=8,'narrow'=2] {'wide','narrow'}, dimensions={0}, use_global_device_ids=true | all-gather | bytes 69632 | tf_op jit(solution)/shard_map/all_gather | solution.py:95
  43.2 1.5 %reshape.147 = bf16[64,512]{1,0:T(8,128)(2,1)} reshape(bf16[16,4,512]{2,1,0:T(4,128)(2,1)} %all-gather) | data formatting | bytes 131072
  44.7 1.6 %fusion.14 = f32[32,512]{1,0:T(8,128)} fusion(bf16[32,512]{1,0:T(8,128)(2,1)} %param.21, bf16[1536,512]{1,0:T(8,128)(2,1)S(1)} %copy-done.2), kind=kOutput, calls=%fused_computation.25 | convolution fusion | flops 16777216 | bytes 622592 | tf_op jit(solution)/shard_map/dot_general | solution.py:102
  46.2 1.2 %fusion.33 = s32[32]{0:T(128)} fusion(s32[32]{0:T(128)} %param.22), kind=kLoop, calls=%fused_computation.67 | loop fusion | flops 448 | bytes 256 | tf_op jit(solution)/shard_map/add | solution.py:94
  47.5 2.1 %fusion.12 = f32[160,512]{1,0:T(8,128)} fusion(bf16[160,512]{1,0:T(8,128)(2,1)} %param.17, bf16[1024,512]{1,0:T(8,128)(2,1)} %param.29), kind=kOutput, calls=%fused_computation.23 | convolution fusion | flops 83886080 | bytes 1015808 | tf_op jit(solution)/shard_map/dot_general | solution.py:114
  49.6 1.3 %gather_fusion.3 = f32[32,512]{1,0:T(8,128)} fusion(f32[160,512]{1,0:T(8,128)S(1)} %fusion.10, s32[1024]{0:T(1024)} %pad_clamp_fusion), kind=kCustom, calls=%fused_computation.3 | custom fusion | bytes 131200 | tf_op jit(solution)/shard_map/gather | solution.py:106
  50.9 1.9 %fusion.1 = f32[32,512]{1,0:T(8,128)} fusion(f32[32,512]{1,0:T(8,128)} %gather_fusion.3, f32[32,512]{1,0:T(8,128)} %fusion.14, bf16[64,512]{1,0:T(8,128)(2,1)} %reshape.147, bf16[1536,512]{1,0:T(8,128)(2,1)S(1)} %copy-done.2, s32[32]{0:T(128)} %fusion.33), kind=kOutput, calls=%fused_computation.13 | convolution fusion | flops 18925568 | bytes 786560 | tf_op jit(solution)/shard_map/dot_general | solution.py:105
  53.5 4.9 %gather_fusion.2 = f32[960,512]{1,0:T(8,128)} fusion(f32[160,512]{1,0:T(8,128)S(1)} %fusion.10, s32[1024]{0:T(1024)S(1)} %pad_clamp_fusion.1), kind=kCustom, calls=%fused_computation.2 | custom fusion | bytes 3936000 | tf_op jit(solution)/shard_map/gather | solution.py:92
  58.4 4.8 %gather_fusion = f32[960,512]{1,0:T(8,128)} fusion(f32[320,512]{1,0:T(8,128)S(1)} %fusion.21, s32[1024]{0:T(1024)S(1)} %pad_clamp_fusion.3), kind=kCustom, calls=%fused_computation | custom fusion | bytes 3936000 | tf_op jit(solution)/shard_map/gather | solution.py:87
  64.1 1.3 %fusion.19 = f32[80,512]{1,0:T(8,128)S(1)} fusion(bf16[1536,512]{1,0:T(8,128)(2,1)} %param.24, bf16[40,512]{1,0:T(8,128)(2,1)} %bitcast.2, bf16[40,512]{1,0:T(8,128)(2,1)} %bitcast.1), kind=kOutput, calls=%fused_computation.30 | convolution fusion | flops 42106880 | bytes 770048 | tf_op jit(solution)/shard_map/dot_general | solution.py:80
  65.5 4.8 %gather_fusion.1 = f32[960,512]{1,0:T(8,128)} fusion(f32[80,512]{1,0:T(8,128)S(1)} %fusion.19, s32[1024]{0:T(1024)S(1)} %pad_clamp_fusion.2), kind=kCustom, calls=%fused_computation.1 | custom fusion | bytes 3936000 | tf_op jit(solution)/shard_map/gather | solution.py:87
  70.3 3.2 %add_add_fusion = f32[960,512]{1,0:T(8,128)S(1)} fusion(f32[960,512]{1,0:T(8,128)} %gather_fusion.2, f32[960,512]{1,0:T(8,128)S(1)} %copy-done.1, f32[960,512]{1,0:T(8,128)} %gather_fusion, f32[960,512]{1,0:T(8,128)} %gather_fusion.1, pred[960]{0:T(1024)(128)(4,1)S(1)} %copy-done.9), kind=kLoop, calls=%fused_computation.8 | loop fusion | flops 1474560 | bytes 9831360 | tf_op jit(solution)/shard_map/add | solution.py:90
  75.4 2.7 %multiply_convert_fusion.2 = bf16[160,512]{1,0:T(8,128)(2,1)} fusion(f32[160,512]{1,0:T(8,128)S(1)} %copy-done.5, bf16[1024,512]{1,0:T(8,128)(2,1)} %param.29, f32[992,512]{1,0:T(8,128)S(1)} %get-tuple-element.10, f32[512]{0:T(512)S(1)} %copy-done.15, f32[512]{0:T(512)S(1)} %copy-done.16, f32[992]{0:T(1024)S(1)} %add_rsqrt_fusion, ...), kind=kOutput, calls=%fused_computation.36 | convolution fusion | flops 249768960 | bytes 3065472 | tf_op jit(solution)/shard_map/dot_general | solution.py:117
  78.0 1.5 %fusion.41 = (f32[160]{0:T(256)S(1)}, f32[160,512]{1,0:T(8,128)S(1)}) fusion(bf16[160,512]{1,0:T(8,128)(2,1)} %multiply_convert_fusion.2, bf16[512,512]{1,0:T(8,128)(2,1)} %param.31), kind=kOutput, calls=%fused_computation.78 | convolution fusion | flops 83967840 | bytes 1016448 | tf_op jit(solution)/shard_map/dot_general | solution.py:30
  79.8 0.8 %add_convert_fusion.3 = bf16[160,512]{1,0:T(8,128)(2,1)} fusion(bf16[160,512]{1,0:T(8,128)(2,1)S(1)} %copy-done.3, f32[160,512]{1,0:T(8,128)S(1)} %get-tuple-element.12, f32[512]{0:T(512)S(1)} %copy-done.11, f32[512]{0:T(512)S(1)} %copy-done.12, f32[160]{0:T(256)S(1)} %add_rsqrt_fusion.1, f32[160]{0:T(256)S(1)} %broadcast_multiply_fusion.1), kind=kLoop, calls=%fused_computation.34 | loop fusion | flops 573440 | bytes 660736 | tf_op jit(solution)/shard_map/convert_element_type | solution.py:122
  (62 shorter events, 7.9 us)
Async XLA Ops:
  0.0 20.7 %copy-start = (bf16[960,512]{1,0:T(8,128)(2,1)S(1)}, bf16[960,512]{1,0:T(8,128)(2,1)}, u32[]{:S(2)}) copy-start(bf16[960,512]{1,0:T(8,128)(2,1)} %param.18) | copy-start | bytes 2949124
  0.0 16.3 %copy-start.2 = (bf16[1536,512]{1,0:T(8,128)(2,1)S(1)}, bf16[1536,512]{1,0:T(8,128)(2,1)}, u32[]{:S(2)}) copy-start(bf16[1536,512]{1,0:T(8,128)(2,1)} %param.24) | copy-start | bytes 4718596
  0.0 17.6 %copy-start.7 = (s32[960]{0:T(1024)S(1)}, s32[960]{0:T(1024)}, u32[]{:S(2)}) copy-start(s32[960]{0:T(1024)} %param.19) | copy-start | bytes 11524
  0.0 20.0 %copy-start.10 = (s32[960]{0:T(1024)S(1)}, s32[960]{0:T(1024)}, u32[]{:S(2)}) copy-start(s32[960]{0:T(1024)} %param.20) | copy-start | bytes 11524
  0.6 62.6 %collective-permute-start.2 = (s32[1,40]{1,0:T(1,128)}, s32[1,40]{1,0:T(1,128)}, u32[]{:S(2)}, u32[]{:S(2)}) collective-permute-start(s32[1,40]{1,0:T(1,128)} %fusion.32), channel_id=1, source_target_pairs={{0,2},{2,4},{4,6},{6,8},{8,10},{10,12},{12,14},{14,0},{1,3},{3,5},... | collective-permute-start | bytes 488 | tf_op jit(solution)/shard_map/ppermute | solution.py:16
  3.5 59.7 %collective-permute-start.3 = (s32[1,40]{1,0:T(1,128)}, s32[1,40]{1,0:T(1,128)}, u32[]{:S(2)}, u32[]{:S(2)}) collective-permute-start(s32[1,40]{1,0:T(1,128)} %fusion.32), channel_id=1, source_target_pairs={{2,0},{4,2},{6,4},{8,6},{10,8},{12,10},{14,12},{0,14},{3,1},{5,3},... | collective-permute-start | bytes 488 | tf_op jit(solution)/shard_map/ppermute | solution.py:17
  8.8 0.7 copy-start.4
  10.2 53.9 %collective-permute-start = (bf16[1,40,512]{2,1,0:T(8,128)(2,1)}, bf16[1,40,512]{2,1,0:T(8,128)(2,1)}, u32[]{:S(2)}, u32[]{:S(2)}) collective-permute-start(bf16[1,40,512]{2,1,0:T(8,128)(2,1)} %broadcast_in_dim_reshape.3), channel_id=1, source_target_pairs={{0,2},{2,4},{4,6},{6,8},{8,10},{10,12},{12,14},{14,0},{1,3},{3,5},... | collective-permute-start | bytes 122888 | tf_op jit(solution)/shard_map/ppermute | solution.py:16
  10.2 53.9 %collective-permute-start.1 = (bf16[1,40,512]{2,1,0:T(8,128)(2,1)}, bf16[1,40,512]{2,1,0:T(8,128)(2,1)}, u32[]{:S(2)}, u32[]{:S(2)}) collective-permute-start(bf16[1,40,512]{2,1,0:T(8,128)(2,1)} %broadcast_in_dim_reshape.3), channel_id=1, source_target_pairs={{2,0},{4,2},{6,4},{8,6},{10,8},{12,10},{14,12},{0,14},{3,1},{5,3},... | collective-permute-start | bytes 122888 | tf_op jit(solution)/shard_map/ppermute | solution.py:17
  20.0 4.5 %copy-start.8 = (bf16[1,4,512]{2,1,0:T(4,128)(2,1)S(1)}, bf16[1,4,512]{2,1,0:T(4,128)(2,1)}, u32[]{:S(2)}) copy-start(bf16[1,4,512]{2,1,0:T(4,128)(2,1)} %slice_bitcast_fusion) | copy-start | bytes 12292
  65.4 4.9 %copy-start.1 = (f32[960,512]{1,0:T(8,128)S(1)}, f32[960,512]{1,0:T(8,128)}, u32[]{:S(2)}) copy-start(f32[960,512]{1,0:T(8,128)} %fusion.16) | copy-start | bytes 5898244
  65.4 4.9 %copy-start.9 = (pred[960]{0:T(1024)(128)(4,1)S(1)}, pred[960]{0:T(1024)(128)(4,1)}, u32[]{:S(2)}) copy-start(pred[960]{0:T(1024)(128)(4,1)} %compare_and_fusion) | copy-start | bytes 2884
  70.3 3.2 %copy-start.6 = (f32[32,512]{1,0:T(8,128)S(1)}, f32[32,512]{1,0:T(8,128)}, u32[]{:S(2)}) copy-start(f32[32,512]{1,0:T(8,128)} %fusion.1) | copy-start | bytes 196612
  70.3 3.2 %copy-start.13 = (bf16[512,512]{1,0:T(8,128)(2,1)S(1)}, bf16[512,512]{1,0:T(8,128)(2,1)}, u32[]{:S(2)}) copy-start(bf16[512,512]{1,0:T(8,128)(2,1)} %param.26) | copy-start | bytes 1572868
  70.3 3.2 %copy-start.14 = (f32[512]{0:T(512)S(1)}, f32[512]{0:T(512)}, u32[]{:S(2)}) copy-start(f32[512]{0:T(512)} %param.25) | copy-start | bytes 6148
  74.4 1.0 %copy-start.5 = (f32[160,512]{1,0:T(8,128)S(1)}, f32[160,512]{1,0:T(8,128)}, u32[]{:S(2)}) copy-start(f32[160,512]{1,0:T(8,128)} %fusion.12) | copy-start | bytes 983044
  74.4 1.0 %copy-start.15 = (f32[512]{0:T(512)S(1)}, f32[512]{0:T(512)}, u32[]{:S(2)}) copy-start(f32[512]{0:T(512)} %param.28) | copy-start | bytes 6148
  74.4 1.0 %copy-start.16 = (f32[512]{0:T(512)S(1)}, f32[512]{0:T(512)}, u32[]{:S(2)}) copy-start(f32[512]{0:T(512)} %param.27) | copy-start | bytes 6148
  74.4 1.0 %copy-start.17 = (f32[512]{0:T(512)S(1)}, f32[512]{0:T(512)}, u32[]{:S(2)}) copy-start(f32[512]{0:T(512)} %param.30) | copy-start | bytes 6148
  75.3 4.4 %copy-start.3 = (bf16[160,512]{1,0:T(8,128)(2,1)S(1)}, bf16[160,512]{1,0:T(8,128)(2,1)}, u32[]{:S(2)}) copy-start(bf16[160,512]{1,0:T(8,128)(2,1)} %param.17) | copy-start | bytes 491524
  75.4 4.4 %copy-start.11 = (f32[512]{0:T(512)S(1)}, f32[512]{0:T(512)}, u32[]{:S(2)}) copy-start(f32[512]{0:T(512)} %param.33) | copy-start | bytes 6148
  75.4 4.4 %copy-start.12 = (f32[512]{0:T(512)S(1)}, f32[512]{0:T(512)}, u32[]{:S(2)}) copy-start(f32[512]{0:T(512)} %param.32) | copy-start | bytes 6148
where the time goes:
time: 81.2 us; the launch traced here: 80.6 us
  blocking collectives  20.9 us (26%)
  local copies, waits for them, and re-layouts  20.6 us (25%)
  matrix products  16.4 us (20%)
  other arithmetic  11.6 us (14%)
  starting transfers between devices  10.7 us (13%)
    all_gather x1, blocking collectives, shards(): lax.all_gather(node_latent[:COARSE_DEV], ('wide', 'narrow'), axis=0, tile...  18.7 us
    ppermute x2, starting transfers between devices, with_halo(): after = lax.ppermute(first, axis, down)  7.76 us
    gather x1, local copies, waits for them, and re-layouts, shards(): node_proj[local_recv]  4.86 us
    gather x1, local copies, waits for them, and re-layouts, shards(): remote_proj[outer_pos]  4.84 us
    gather x1, local copies, waits for them, and re-layouts, shards(): patch_proj[inner_pos]  4.82 us
    unnamed x38, local copies, waits for them, and re-layouts  4.08 us
    add x1, other arithmetic, shards(): jnp.dot(fine_edges, w_edge, preferred_element_type=jnp.float32)  3.19 us
    ppermute x2, starting transfers between devices, with_halo(): before = lax.ppermute(last, axis, up)  2.98 us
  transfers between devices with their start and end apart: 4, of which 0 were waited for; matrix products, arithmetic and copies ran while one was open for 39% of the time, Pallas kernels for 0%

commit v1 on v0

v1 whole, which is shorter than its diff:
```python
import functools

import jax
import jax.numpy as jnp
from jax import lax
from jax.experimental import pallas as pl
from jax.experimental.pallas import tpu as pltpu
from jax.sharding import PartitionSpec as P

COARSE_DEV = 4
LANES = 128
BF16 = jnp.bfloat16
F32 = jnp.float32


def silu(v):
    u = v * 0.5
    return u + u * jnp.tanh(u)


def layer_norm(values, gain_row, shift_row):
    center = values - jnp.mean(values, axis=-1, keepdims=True)
    spread = jnp.mean(center * center, axis=-1, keepdims=True)
    return center * lax.rsqrt(spread + 1e-05) * gain_row + shift_row


def dot(a, b):
    return jnp.dot(a, b, preferred_element_type=F32)


def columns(row):
    return jnp.broadcast_to(row, (LANES, row.shape[1])).T


def one_hot(cols, width):
    lane = lax.broadcasted_iota(jnp.int32, cols[0].shape, 1)
    blocks = []
    for b in range(width // LANES):
        hit = cols[0] == lane + b * LANES
        for c in cols[1:]:
            hit = hit | (c == lane + b * LANES)
        blocks.append(jnp.where(hit, 1.0, 0.0).astype(BF16))
    return jnp.concatenate(blocks, axis=1)


def local_kernel(
    nodes, halo, n_patches,
    nl, fe, ce, fs, fr, cs, cr, w_in, e_bias, u_in, n_bias,
    base_f, base_c, oh2, sel, inc_f, inc_c, nu, table,
):
    d = nl.shape[1]
    wide = lax.axis_index("wide")
    half = lax.axis_index("narrow")
    device = wide * 2 + half
    x_patch = wide ^ 1
    y_patch = jnp.where(wide % 2 == 0, wide + n_patches - 1, wide + 1) % n_patches
    patch = 2 * nodes
    first = nodes - halo
    block = halo + COARSE_DEV

    node_rows = nl[...]
    table[0:nodes, :] = dot(node_rows, w_in[2 * d : 3 * d, :]).astype(BF16)
    table[nodes : 2 * nodes, :] = dot(node_rows, w_in[d : 2 * d, :]).astype(BF16)
    table[2 * nodes :, :] = jnp.zeros_like(table[2 * nodes :, :])
    nu[...] = dot(node_rows, u_in[0:d, :]) + n_bias[...]

    recv = fr[...] - device * nodes
    send = fs[...]

    def offset(p):
        off = send - p * patch
        inside = (off >= 0) & (off < patch)
        upper = (off >= nodes).astype(jnp.int32)
        return inside, upper, off - upper * nodes

    inside, upper, loc = offset(wide)
    own = jnp.where(inside & (upper == half), loc + nodes, -1)
    pos = jnp.where(inside & (upper != half), loc, -1)
    for k, p in enumerate((x_patch, y_patch)):
        inside, upper, loc = offset(p)
        slot = jnp.where(upper == half, 0, 1)
        at = nodes + k * 2 * block + slot * block + loc - first
        pos = jnp.where(inside, at, pos)

    recv_c = cr[...] - device * nodes
    chip_rows = cs[...].astype(F32)
    owner = jnp.floor((chip_rows + 0.5) * (1.0 / nodes)).astype(jnp.int32)
    slot_c = cs[...] - owner * nodes
    pos_c = ((owner // 2) ^ wide) * (2 * COARSE_DEV) + ((owner % 2) ^ half) * COARSE_DEV + slot_c

    node_at = lax.broadcasted_iota(jnp.int32, (nodes, fr.shape[1]), 0)
    inc_f[...] = jnp.where(node_at == recv, 1.0, 0.0).astype(BF16)
    node_at = lax.broadcasted_iota(jnp.int32, (nodes, cr.shape[1]), 0)
    inc_c[...] = jnp.where(node_at == recv_c, 1.0, 0.0).astype(BF16)

    wide_c = -(-sel.shape[1] // LANES) * LANES
    sel[...] = one_hot((columns(pos_c),), wide_c)[:, : sel.shape[1]]
    oh_c = one_hot((columns(recv_c),), table.shape[0])
    base_c[...] = dot(ce[...], w_in[0:d, :]) + dot(oh_c, table[...]) + e_bias[...]

    recv_cols, own_cols, pos_cols = columns(recv), columns(own), columns(pos)
    oh2[...] = one_hot((pos_cols,), oh2.shape[1])
    rows = fe.shape[0]
    step = rows // 4
    for at in range(0, rows, step):
        s = slice(at, at + step)
        oh1 = one_hot((recv_cols[s], own_cols[s]), table.shape[0])
        base_f[s, :] = dot(fe[s, :], w_in[0:d, :]) + dot(oh1, table[...]) + e_bias[...]


def main_kernel(
    partner, x_rows, y_rows, coarse, nl, base_f, base_c, oh2, sel, inc_f, inc_c, nu,
    w_in, w_out, e_gain, e_shift, u_in, u_out, n_gain, n_shift,
    out, table,
):
    d = nl.shape[1]
    w_send = w_in[d : 2 * d, :]
    a = partner.shape[0]
    b = a + x_rows.shape[0]
    table[0:a, :] = dot(partner[...], w_send).astype(BF16)
    table[a:b, :] = dot(x_rows[...], w_send).astype(BF16)
    table[b:, :] = dot(y_rows[...], w_send).astype(BF16)

    def messages(pre):
        edge_out = dot(silu(pre).astype(BF16), w_out[...])
        return layer_norm(edge_out, e_gain[...], e_shift[...]).astype(BF16)

    picked = dot(sel[...], coarse[...]).astype(BF16)
    summed = dot(inc_c[...], messages(base_c[...] + dot(picked, w_send)))
    rows = base_f.shape[0]
    for at in range(0, rows, 256):
        s = slice(at, min(at + 256, rows))
        pre = base_f[s, :] + dot(oh2[s, :], table[...])
        summed = summed + dot(inc_f[:, s], messages(pre))
    pre = nu[...] + dot(summed.astype(BF16), u_in[d : 2 * d, :])
    update = dot(silu(pre).astype(BF16), u_out[...])
    update = layer_norm(update, n_gain[...], n_shift[...])
    out[...] = (nl[...].astype(F32) + update).astype(BF16)


def vmem(n):
    return [pl.BlockSpec(memory_space=pltpu.VMEM)] * n


def shards(
    node_latent, fine_edges, fine_senders, fine_receivers, coarse_edges, coarse_senders,
    coarse_receivers, edge_weight_in, edge_bias, edge_weight_out, edge_gain, edge_shift,
    node_weight_in, node_bias, node_weight_out, node_gain, node_shift,
):
    nodes, d = node_latent.shape
    halo = nodes // 8
    n_patches = lax.axis_size("wide")
    edges, coarse_count = fine_edges.shape[0], coarse_edges.shape[0]
    row = lambda v: v.reshape(1, -1)

    partner = lax.ppermute(node_latent, "narrow", [(0, 1), (1, 0)])
    pay = jnp.concatenate(
        [node_latent[nodes - halo :], node_latent[:COARSE_DEV], partner[nodes - halo :], partner[:COARSE_DEV]],
        axis=0,
    )
    around = range(n_patches)
    x_rows = lax.ppermute(pay, "wide", [(i, i ^ 1) for i in around])
    y_rows = lax.ppermute(
        pay, "wide", [(i, (i - 1 if i % 2 == 0 else i + 1) % n_patches) for i in around]
    )
    block = halo + COARSE_DEV
    known = jnp.concatenate(
        [pay[halo:block], pay[halo + block :], x_rows[halo:block], x_rows[halo + block :]], axis=0
    )
    have = 2
    while have < n_patches:
        parts = [known]
        for k in range(1, min(4, n_patches // have)):
            parts.append(lax.ppermute(known, "wide", [(i, i ^ (k * have)) for i in around]))
        known = jnp.concatenate(parts, axis=0)
        have *= len(parts)

    table_a = -(-2 * nodes // LANES) * LANES
    table_b = nodes + 4 * block
    shape = jax.ShapeDtypeStruct
    local_out = pl.pallas_call(
        functools.partial(local_kernel, nodes, halo, n_patches),
        out_shape=(
            shape((edges, d), F32),
            shape((coarse_count, d), F32),
            shape((edges, table_b), BF16),
            shape((coarse_count, known.shape[0]), BF16),
            shape((nodes, edges), BF16),
            shape((nodes, coarse_count), BF16),
            shape((nodes, d), F32),
        ),
        in_specs=vmem(11),
        out_specs=tuple(vmem(7)),
        scratch_shapes=[pltpu.VMEM((table_a, d), BF16)],
        name="local",
    )(
        node_latent, fine_edges, coarse_edges, row(fine_senders), row(fine_receivers),
        row(coarse_senders), row(coarse_receivers), edge_weight_in, row(edge_bias),
        node_weight_in, row(node_bias),
    )
    return pl.pallas_call(
        main_kernel,
        out_shape=shape((nodes, d), BF16),
        in_specs=vmem(20),
        out_specs=pl.BlockSpec(memory_space=pltpu.VMEM),
        scratch_shapes=[pltpu.VMEM((table_b, d), BF16)],
        name="main",
    )(
        partner, x_rows, y_rows, known, node_latent, *local_out,
        edge_weight_in, edge_weight_out, row(edge_gain), row(edge_shift),
        node_weight_in, node_weight_out, row(node_gain), row(node_shift),
    )


def solution(mesh):
    axes = ("grp", "wide", "narrow")
    matrix, vector, whole = P(axes, None), P(axes), P()
    return jax.shard_map(
        shards,
        mesh=mesh,
        in_specs=(matrix, matrix, vector, vector, matrix, vector, vector) + (whole,) * 10,
        out_specs=matrix,
        check_vma=False,
    )
```

time: 81.2 us -> 29.9 us (0.37)
  blocking collectives: 20.9 us -> 0 us
  matrix products: 16.4 us -> 0 us
  local copies, waits for them, and re-layouts: 20.6 us -> 5.13 us
  Pallas kernels: 0 us -> 13.2 us
  other arithmetic: 11.6 us -> 0.04 us
    all_gather x2 -> x0, blocking collectives: 20.9 us -> none  [the longest x1 18.7 us: shards(): lax.all_gather(node_latent[:COARSE_DEV], ('wide', 'narrow'), axis=0, tile...]
    dot_general x10 -> x0, matrix products: 16.4 us -> none  [the longest x1 2.65 us: shards(): jnp.dot(summed, node_weight_in[latent_width:], preferred_element_type=jnp...]
    gather x4 -> x0, local copies, waits for them, and re-layouts: 15.9 us -> none  [the longest x1 4.86 us: shards(): node_proj[local_recv]]
    pallas_call x0 -> x2, Pallas kernels: none -> 13.2 us  [the longest x1 7.82 us: shards(): pl.pallas_call(main_kernel, out_shape=shape((nodes, d), BF16), in_specs=v...]
    add x3 -> x0, other arithmetic: 4.98 us -> none  [the longest x1 3.19 us: shards(): jnp.dot(fine_edges, w_edge, preferred_element_type=jnp.float32)]
    unnamed x38 -> x6, local copies, waits for them, and re-layouts: 4.08 us -> 0.62 us
    concatenate x0 -> x1, local copies, waits for them, and re-layouts: none -> 3.04 us  [shards(): known = jnp.concatenate(parts, axis=0)]
    select_n x4 -> x0, other arithmetic: 1.8 us -> none  [the longest x1 1.19 us: shards(): node_proj[coarse_local]]
  transfers between devices with their start and end apart: 4 -> 6, of which waited for: 0 -> 0; matrix products, arithmetic and copies ran while one was open for 39% -> 15% of each run, Pallas kernels for 0% -> 18%
where the time goes in v1:
time: 29.9 us; the launch traced here: 29.6 us
  Pallas kernels  13.2 us (44%)
  starting transfers between devices  11.2 us (37%)
  local copies, waits for them, and re-layouts  5.13 us (17%)
    pallas_call x1, Pallas kernels, shards(): pl.pallas_call(main_kernel, out_shape=shape((nodes, d), BF16), in_specs=v...  7.82 us
    pallas_call x1, Pallas kernels, shards(): pl.pallas_call(functools.partial(local_kernel, nodes, halo, n_patches), o...  5.37 us
    ppermute x3, starting transfers between devices, shards(): lax.ppermute(known, 'wide', [(i, i ^ k * have) for i in around])  4.45 us
    ppermute x1, starting transfers between devices, shards(): lax.ppermute(pay, 'wide', [(i, (i - 1 if i % 2 == 0 else i + 1) % n_patch...  3.57 us
    concatenate x1, local copies, waits for them, and re-layouts, shards(): known = jnp.concatenate(parts, axis=0)  3.04 us
    ppermute x1, starting transfers between devices, shards(): x_rows = lax.ppermute(pay, 'wide', [(i, i ^ 1) for i in around])  2.67 us
    slice x1, local copies, waits for them, and re-layouts, shards(): node_latent[nodes - halo:]  0.75 us
    slice x1, local copies, waits for them, and re-layouts, shards(): node_latent[:COARSE_DEV]  0.7 us
  transfers between devices with their start and end apart: 6, of which 0 were waited for; matrix products, arithmetic and copies ran while one was open for 15% of the time, Pallas kernels for 18%

profile of v1, /device:TPU:0, one launch (start us, length us, event | category | flops | bytes accessed | tf_op | source)
XLA Modules:
  0.0 29.6 jit_solution(9931870451423009420)
XLA Ops:
  0.0 0.5 %collective-permute-start = (bf16[160,512]{1,0:T(8,128)(2,1)}, bf16[160,512]{1,0:T(8,128)(2,1)S(1)}, u32[]{:S(2)}, u32[]{:S(2)}) collective-permute-start(bf16[160,512]{1,0:T(8,128)(2,1)} %nl.3), channel_id=1, source_target_pairs={{0,1},{1,0},{2,3},{3,2},{4,5},{5,4},{6,7},{7,6},{8,9},{9,8},{10,11... | collective-permute-start | bytes 491528 | tf_op jit(solution)/shard_map/ppermute | solution.py:156
  0.5 0.7 %slice.19 = bf16[4,512]{1,0:T(4,128)(2,1)S(1)} slice(bf16[160,512]{1,0:T(8,128)(2,1)} %nl.3), slice={[0:4], [0:512]} | slice | bytes 8192 | tf_op jit(solution)/shard_map/slice | solution.py:158
  1.2 0.7 %slice.18 = bf16[20,512]{1,0:T(8,128)(2,1)S(1)} slice(bf16[160,512]{1,0:T(8,128)(2,1)} %nl.3), slice={[140:160], [0:512]} | slice | bytes 40960 | tf_op jit(solution)/shard_map/slice | solution.py:158
  1.9 0.0 collective-permute-done.partner
  1.9 0.0 copy-start
  2.0 2.7 %collective-permute-start.1 = (bf16[48,512]{1,0:T(8,128)(2,1)S(1)}, bf16[48,512]{1,0:T(8,128)(2,1)S(1)}, u32[]{:S(2)}, u32[]{:S(2)}) collective-permute-start(bf16[48,512]{1,0:T(8,128)(2,1)S(1)} %pad_maximum_fusion), channel_id=1, source_target_pairs={{0,2},{2,0},{4,6},{6,4},{8,10},{10,8},{12,14},{14,12},{1,3},{3,1},... | collective-permute-start | bytes 147464 | tf_op jit(solution)/shard_map/ppermute | solution.py:162
  4.7 3.6 %collective-permute-start.2 = (bf16[48,512]{1,0:T(8,128)(2,1)S(1)}, bf16[48,512]{1,0:T(8,128)(2,1)S(1)}, u32[]{:S(2)}, u32[]{:S(2)}) collective-permute-start(bf16[48,512]{1,0:T(8,128)(2,1)S(1)} %pad_maximum_fusion), channel_id=1, source_target_pairs={{0,14},{2,4},{4,2},{6,8},{8,6},{10,12},{12,10},{14,0},{1,15},{3,5}... | collective-permute-start | bytes 147464 | tf_op jit(solution)/shard_map/ppermute | solution.py:163
  8.3 0.0 collective-permute-done.1.x_rows
  8.3 0.0 copy-start.1
  8.3 2.7 %collective-permute-start.5 = (bf16[16,512]{1,0:T(8,128)(2,1)S(1)}, bf16[16,512]{1,0:T(8,128)(2,1)S(1)}, u32[]{:S(2)}, u32[]{:S(2)}) collective-permute-start(bf16[16,512]{1,0:T(8,128)(2,1)S(1)} %pad_maximum_fusion.1), channel_id=1, source_target_pairs={{0,12},{2,14},{4,8},{6,10},{8,4},{10,6},{12,0},{14,2},{1,13},{3,15... | collective-permute-start | bytes 49160 | tf_op jit(solution)/shard_map/ppermute | solution.py:174
  11.0 0.0 collective-permute-start.4
  11.0 1.8 %collective-permute-start.3 = (bf16[16,512]{1,0:T(8,128)(2,1)S(1)}, bf16[16,512]{1,0:T(8,128)(2,1)S(1)}, u32[]{:S(2)}, u32[]{:S(2)}) collective-permute-start(bf16[16,512]{1,0:T(8,128)(2,1)S(1)} %pad_maximum_fusion.1), channel_id=1, source_target_pairs={{0,4},{2,6},{4,0},{6,2},{8,12},{10,14},{12,8},{14,10},{1,5},{3,7},... | collective-permute-start | bytes 49160 | tf_op jit(solution)/shard_map/ppermute | solution.py:174
  12.8 5.4 %local.1 = (f32[960,512]{1,0:T(8,128)}, f32[32,512]{1,0:T(8,128)}, bf16[960,256]{1,0:T(8,128)(2,1)}, bf16[32,64]{1,0:T(8,128)(2,1)}, bf16[160,960]{1,0:T(8,128)(...) custom-call(bf16[160,512]{1,0:T(8,128)(2,1)} %nl.3, bf16[960,512]{1,0:T(8,128)(2,1)} %fe.1, bf16[32,512]{1,0:T(8,128)(2,1)} %ce.1, ...), custom_call_target="tpu_custom_call" | custom-call | tf_op jit(solution)/shard_map/local/pallas_call | solution.py:181
  18.1 0.0 copy-done
  18.1 0.0 collective-permute-done.5
  18.1 0.0 collective-permute-done.4
  18.1 0.0 collective-permute-done.3
  18.2 3.0 %concatenate.12.coarse = bf16[64,512]{1,0:T(8,128)(2,1)} concatenate(bf16[4,512]{1,0:T(4,128)(2,1)S(1)} %slice.19, bf16[4,512]{1,0:T(4,128)(2,1)S(1)} %slice.25, bf16[4,512]{1,0:T(4,128)(2,1)S(1)} %get-tuple-element.20, bf16[4,512]{1,0:T(4,128)(2,1)S(1)} %get-tuple-element.19, bf16[16,512]{1,0:T(8,128)(2,1)S(1)} %collective-permute-done.3, ...), dimensions={0} | concatenate | bytes 131072 | tf_op jit(solution)/shard_map/concatenate | solution.py:175
  21.2 0.0 copy-done.1
  21.2 0.0 collective-permute-done.2.y_rows
  21.2 0.0 copy-start.2
  21.2 0.6 %copy-done.2 = bf16[48,512]{1,0:T(8,128)(2,1)} copy-done((bf16[48,512]{1,0:T(8,128)(2,1)}, bf16[48,512]{1,0:T(8,128)(2,1)S(1)}, u32[]{:S(2)}) %copy-start.2) | copy-done | bytes 49176
  21.8 7.8 %main.1 = bf16[160,512]{1,0:T(8,128)(2,1)} custom-call(bf16[160,512]{1,0:T(8,128)(2,1)} %copy-done, bf16[48,512]{1,0:T(8,128)(2,1)} %copy-done.1, bf16[48,512]{1,0:T(8,128)(2,1)} %copy-done.2, bf16[64,512]{1,0:T(8,128)(2,1)} %concatenate.12.coarse, bf16[160,512]{1,0:T(8,128)(2,1)} %nl.3, f32[960,512]{1,0:T(8,128)} %get-tuple-element.12.base_f, ...), custom_call_target="tpu_custom_call" | custom-call | tf_op jit(solution)/shard_map/main/pallas_call | solution.py:201
  (5 shorter events, 0.1 us)
Async XLA Ops:
  0.0 1.9 %collective-permute-start = (bf16[160,512]{1,0:T(8,128)(2,1)}, bf16[160,512]{1,0:T(8,128)(2,1)S(1)}, u32[]{:S(2)}, u32[]{:S(2)}) collective-permute-start(bf16[160,512]{1,0:T(8,128)(2,1)} %nl.3), channel_id=1, source_target_pairs={{0,1},{1,0},{2,3},{3,2},{4,5},{5,4},{6,7},{7,6},{8,9},{9,8},{10,11... | collective-permute-start | bytes 491528 | tf_op jit(solution)/shard_map/ppermute | solution.py:156
  1.9 16.2 %copy-start = (bf16[160,512]{1,0:T(8,128)(2,1)}, bf16[160,512]{1,0:T(8,128)(2,1)S(1)}, u32[]{:S(2)}) copy-start(bf16[160,512]{1,0:T(8,128)(2,1)S(1)} %collective-permute-done.partner) | copy-start | bytes 491524
  2.0 6.2 %collective-permute-start.1 = (bf16[48,512]{1,0:T(8,128)(2,1)S(1)}, bf16[48,512]{1,0:T(8,128)(2,1)S(1)}, u32[]{:S(2)}, u32[]{:S(2)}) collective-permute-start(bf16[48,512]{1,0:T(8,128)(2,1)S(1)} %pad_maximum_fusion), channel_id=1, source_target_pairs={{0,2},{2,0},{4,6},{6,4},{8,10},{10,8},{12,14},{14,12},{1,3},{3,1},... | collective-permute-start | bytes 147464 | tf_op jit(solution)/shard_map/ppermute | solution.py:162
  4.7 16.5 %collective-permute-start.2 = (bf16[48,512]{1,0:T(8,128)(2,1)S(1)}, bf16[48,512]{1,0:T(8,128)(2,1)S(1)}, u32[]{:S(2)}, u32[]{:S(2)}) collective-permute-start(bf16[48,512]{1,0:T(8,128)(2,1)S(1)} %pad_maximum_fusion), channel_id=1, source_target_pairs={{0,14},{2,4},{4,2},{6,8},{8,6},{10,12},{12,10},{14,0},{1,15},{3,5}... | collective-permute-start | bytes 147464 | tf_op jit(solution)/shard_map/ppermute | solution.py:163
  8.3 12.9 %copy-start.1 = (bf16[48,512]{1,0:T(8,128)(2,1)}, bf16[48,512]{1,0:T(8,128)(2,1)S(1)}, u32[]{:S(2)}) copy-start(bf16[48,512]{1,0:T(8,128)(2,1)S(1)} %collective-permute-done.1.x_rows) | copy-start | bytes 147460
  8.3 9.8 %collective-permute-start.5 = (bf16[16,512]{1,0:T(8,128)(2,1)S(1)}, bf16[16,512]{1,0:T(8,128)(2,1)S(1)}, u32[]{:S(2)}, u32[]{:S(2)}) collective-permute-start(bf16[16,512]{1,0:T(8,128)(2,1)S(1)} %pad_maximum_fusion.1), channel_id=1, source_target_pairs={{0,12},{2,14},{4,8},{6,10},{8,4},{10,6},{12,0},{14,2},{1,13},{3,15... | collective-permute-start | bytes 49160 | tf_op jit(solution)/shard_map/ppermute | solution.py:174
  11.0 7.2 %collective-permute-start.4 = (bf16[16,512]{1,0:T(8,128)(2,1)S(1)}, bf16[16,512]{1,0:T(8,128)(2,1)S(1)}, u32[]{:S(2)}, u32[]{:S(2)}) collective-permute-start(bf16[16,512]{1,0:T(8,128)(2,1)S(1)} %pad_maximum_fusion.1), channel_id=1, source_target_pairs={{0,8},{2,10},{4,12},{6,14},{8,0},{10,2},{12,4},{14,6},{1,9},{3,11}... | collective-permute-start | bytes 49160 | tf_op jit(solution)/shard_map/ppermute | solution.py:174
  11.0 7.2 %collective-permute-start.3 = (bf16[16,512]{1,0:T(8,128)(2,1)S(1)}, bf16[16,512]{1,0:T(8,128)(2,1)S(1)}, u32[]{:S(2)}, u32[]{:S(2)}) collective-permute-start(bf16[16,512]{1,0:T(8,128)(2,1)S(1)} %pad_maximum_fusion.1), channel_id=1, source_target_pairs={{0,4},{2,6},{4,0},{6,2},{8,12},{10,14},{12,8},{14,10},{1,5},{3,7},... | collective-permute-start | bytes 49160 | tf_op jit(solution)/shard_map/ppermute | solution.py:174
  21.2 0.6 %copy-start.2 = (bf16[48,512]{1,0:T(8,128)(2,1)}, bf16[48,512]{1,0:T(8,128)(2,1)S(1)}, u32[]{:S(2)}) copy-start(bf16[48,512]{1,0:T(8,128)(2,1)S(1)} %collective-permute-done.2.y_rows) | copy-start | bytes 147460

commit v2 on v1

v2 whole, which is shorter than its diff:
```python
import functools

import jax
import jax.numpy as jnp
from jax import lax
from jax.experimental import pallas as pl
from jax.experimental.pallas import tpu as pltpu
from jax.sharding import PartitionSpec as P

COARSE_DEV = 4
LANES = 128
TAIL = 16
BF16 = jnp.bfloat16
F32 = jnp.float32
MIB = 1 << 20


def silu(v):
    u = v * 0.5
    return u + u * jnp.tanh(u)


def layer_norm(values, gain_row, shift_row):
    center = values - jnp.mean(values, axis=-1, keepdims=True)
    spread = jnp.mean(center * center, axis=-1, keepdims=True)
    return center * lax.rsqrt(spread + 1e-05) * gain_row + shift_row


def dot(a, b):
    return jnp.dot(a, b, preferred_element_type=F32)


def columns(row):
    return jnp.broadcast_to(row, (LANES, row.shape[1])).T


def one_hot(cols, width):
    lane = lax.broadcasted_iota(jnp.int32, cols[0].shape, 1)
    blocks = []
    for b in range(width // LANES):
        hit = cols[0] == lane + b * LANES
        for c in cols[1:]:
            hit = hit | (c == lane + b * LANES)
        blocks.append(jnp.where(hit, 1.0, 0.0).astype(BF16))
    return jnp.concatenate(blocks, axis=1)


def stage_kernel(*refs):
    n = len(refs) // 2
    sems = refs[2 * n]
    copies = [pltpu.make_async_copy(refs[k], refs[n + k], sems.at[k]) for k in range(n)]
    for c in copies:
        c.start()
    for c in copies:
        c.wait()


def pay_kernel(halo, nl, partner, pay):
    nodes = nl.shape[0]
    pay[...] = jnp.concatenate(
        [nl[nodes - halo :, :], nl[:COARSE_DEV, :], partner[nodes - halo :, :], partner[:COARSE_DEV, :]],
        axis=0,
    )


def pair_kernel(halo, pay, x_rows, known):
    block = halo + COARSE_DEV
    known[...] = jnp.concatenate(
        [r[s : s + COARSE_DEV, :] for r in (pay, x_rows) for s in (halo, block + halo)], axis=0
    )


def join_kernel(*refs):
    at = 0
    for r in refs[:-1]:
        refs[-1][at : at + r.shape[0], :] = r[...]
        at += r.shape[0]


def local_kernel(
    nodes, halo, n_patches,
    nl, fs, fr, cs, cr, e_bias, n_bias, fe_hbm, ce_hbm, w_in, w_out_hbm, u_in, u_out_hbm,
    base_f, base_c, oh2, sel, inc_f, inc_c, nu, w_send, w_out, u_mess, u_out,
    table, fe, ce, w_edge, w_recv, u_node, sems,
):
    d = nl.shape[1]
    rows = fe.shape[0]
    step = rows // 4
    moves = [
        (w_in.at[2 * d : 3 * d, :], w_recv),
        (w_in.at[d : 2 * d, :], w_send),
        (w_in.at[0:d, :], w_edge),
        (ce_hbm, ce),
    ]
    moves += [(fe_hbm.at[k * step : (k + 1) * step, :], fe.at[k * step : (k + 1) * step, :]) for k in range(4)]
    moves += [
        (u_in.at[0:d, :], u_node),
        (w_out_hbm, w_out),
        (u_in.at[d : 2 * d, :], u_mess),
        (u_out_hbm, u_out),
    ]
    copies = [pltpu.make_async_copy(src, dst, sems.at[k]) for k, (src, dst) in enumerate(moves)]
    for c in copies:
        c.start()

    wide = lax.axis_index("wide")
    half = lax.axis_index("narrow")
    device = wide * 2 + half
    x_patch = wide ^ 1
    y_patch = jnp.where(wide % 2 == 0, wide + n_patches - 1, wide + 1) % n_patches
    patch = 2 * nodes
    first = nodes - halo
    block = halo + COARSE_DEV

    recv = fr[...] - device * nodes
    send = fs[...]

    def offset(p):
        off = send - p * patch
        inside = (off >= 0) & (off < patch)
        upper = (off >= nodes).astype(jnp.int32)
        return inside, upper, off - upper * nodes

    inside, upper, loc = offset(wide)
    own = jnp.where(inside & (upper == half), loc + nodes, -1)
    pos = jnp.where(inside & (upper != half), loc, -1)
    for k, p in enumerate((x_patch, y_patch)):
        inside, upper, loc = offset(p)
        slot = jnp.where(upper == half, 0, 1)
        at = nodes + k * 2 * block + slot * block + loc - first
        pos = jnp.where(inside, at, pos)

    recv_c = cr[...] - device * nodes
    chip_rows = cs[...].astype(F32)
    owner = jnp.floor((chip_rows + 0.5) * (1.0 / nodes)).astype(jnp.int32)
    slot_c = cs[...] - owner * nodes
    pos_c = ((owner // 2) ^ wide) * (2 * COARSE_DEV) + ((owner % 2) ^ half) * COARSE_DEV + slot_c

    node_at = lax.broadcasted_iota(jnp.int32, (nodes, fr.shape[1]), 0)
    inc_f[...] = jnp.where(node_at == recv, 1.0, 0.0).astype(BF16)
    node_at = lax.broadcasted_iota(jnp.int32, inc_c.shape, 0)
    inc_c[...] = jnp.where(node_at == recv_c, 1.0, 0.0).astype(BF16)
    wide_c = -(-sel.shape[1] // LANES) * LANES
    sel[...] = one_hot((columns(pos_c),), wide_c)[:, : sel.shape[1]]
    oh_c = one_hot((columns(recv_c),), table.shape[0])
    recv_cols, own_cols, pos_cols = columns(recv), columns(own), columns(pos)
    oh2[...] = one_hot((pos_cols,), oh2.shape[1])
    table[2 * nodes :, :] = jnp.zeros_like(table[2 * nodes :, :])

    node_rows = nl[...]
    copies[0].wait()
    table[0:nodes, :] = dot(node_rows, w_recv[...]).astype(BF16)
    copies[1].wait()
    table[nodes : 2 * nodes, :] = dot(node_rows, w_send[...]).astype(BF16)
    copies[2].wait()
    copies[3].wait()
    base_c[...] = dot(ce[...], w_edge[...]) + dot(oh_c, table[...]) + e_bias[...]
    for k in range(4):
        s = slice(k * step, (k + 1) * step)
        copies[4 + k].wait()
        oh1 = one_hot((recv_cols[s], own_cols[s]), table.shape[0])
        base_f[s, :] = dot(fe[s, :], w_edge[...]) + dot(oh1, table[...]) + e_bias[...]
    copies[8].wait()
    nu[...] = dot(node_rows, u_node[...]) + n_bias[...]
    for c in copies[9:]:
        c.wait()


def messages(pre, w_out, e_gain, e_shift):
    edge_out = dot(silu(pre).astype(BF16), w_out[...])
    return layer_norm(edge_out, e_gain[...], e_shift[...]).astype(BF16)


def node_rows_out(own, pre_own, summed, u_mess, u_out, n_gain, n_shift):
    pre = pre_own + dot(summed.astype(BF16), u_mess[...])
    update = dot(silu(pre).astype(BF16), u_out[...])
    update = layer_norm(update, n_gain[...], n_shift[...])
    return (own.astype(F32) + update).astype(BF16)


def fine_kernel(
    partner, x_rows, y_rows, nl, base_f, oh2, inc_f, nu, w_send, w_out, u_mess, u_out,
    e_gain, e_shift, n_gain, n_shift,
    out, head, table,
):
    a = partner.shape[0]
    b = a + x_rows.shape[0]
    table[0:a, :] = dot(partner[...], w_send[...]).astype(BF16)
    table[a:b, :] = dot(x_rows[...], w_send[...]).astype(BF16)
    table[b:, :] = dot(y_rows[...], w_send[...]).astype(BF16)
    rows = base_f.shape[0]
    summed = jnp.zeros(nl.shape, F32)
    for at in range(0, rows, 256):
        s = slice(at, min(at + 256, rows))
        pre = base_f[s, :] + dot(oh2[s, :], table[...])
        summed = summed + dot(inc_f[:, s], messages(pre, w_out, e_gain, e_shift))
    head[...] = summed[:TAIL, :]
    out[...] = node_rows_out(nl[...], nu[...], summed, u_mess, u_out, n_gain, n_shift)


def coarse_kernel(
    n_pieces, out_f, head, nl, nu, base_c, sel, inc_c, w_send, w_out, u_mess, u_out,
    e_gain, e_shift, n_gain, n_shift, *rest,
):
    pieces, (out, rows) = rest[:n_pieces], rest[n_pieces:]
    at = 0
    for r in pieces:
        rows[at : at + r.shape[0], :] = r[...]
        at += r.shape[0]
    picked = dot(sel[...], rows[...]).astype(BF16)
    pre = base_c[...] + dot(picked, w_send[...])
    summed = head[...] + dot(inc_c[...], messages(pre, w_out, e_gain, e_shift))
    out[TAIL:, :] = out_f[TAIL:, :]
    out[:TAIL, :] = node_rows_out(nl[:TAIL, :], nu[:TAIL, :], summed, u_mess, u_out, n_gain, n_shift)


NEAR = pl.BlockSpec(memory_space=pltpu.VMEM)
FAR = pl.BlockSpec(memory_space=pltpu.HBM)


def near(*arrays):
    return [pltpu.with_memory_space_constraint(a, pltpu.VMEM) for a in arrays]


def call(kernel, near_in, outs, name, far_in=(), scratch=(), limit=8, far_out=False, cost=None):
    outs = [(o.shape, o.dtype) if hasattr(o, "shape") else o for o in outs]
    kind = (lambda s, t: jax.ShapeDtypeStruct(s, t)) if far_out else (lambda s, t: pltpu.VMEM(s, t))
    return pl.pallas_call(
        kernel,
        out_shape=tuple(kind(*o) for o in outs),
        in_specs=[NEAR] * len(near_in) + [FAR] * len(far_in),
        out_specs=tuple([NEAR] * len(outs)),
        scratch_shapes=list(scratch),
        compiler_params=pltpu.CompilerParams(vmem_limit_bytes=limit * MIB),
        cost_estimate=pl.CostEstimate(flops=cost or 0, bytes_accessed=cost or 0, transcendentals=0),
        name=name,
    )(*near(*near_in), *[pltpu.with_memory_space_constraint(a, pltpu.HBM) for a in far_in])


def shards(
    node_latent, fine_edges, fine_senders, fine_receivers, coarse_edges, coarse_senders,
    coarse_receivers, edge_weight_in, edge_bias, edge_weight_out, edge_gain, edge_shift,
    node_weight_in, node_bias, node_weight_out, node_gain, node_shift,
):
    nodes, d = node_latent.shape
    halo = nodes // 8
    block = halo + COARSE_DEV
    n_patches = lax.axis_size("wide")
    edges, coarse_count = fine_edges.shape[0], coarse_edges.shape[0]
    small = [node_latent] + [
        v.reshape(1, -1)
        for v in (
            fine_senders, fine_receivers, coarse_senders, coarse_receivers, edge_bias, node_bias,
            edge_gain, edge_shift, node_gain, node_shift,
        )
    ]
    dma = pltpu.SemaphoreType.DMA

    partner = lax.ppermute(node_latent, "narrow", [(0, 1), (1, 0)])
    nl, fs, fr, cs, cr, e_bias, n_bias, e_gain, e_shift, n_gain, n_shift = call(
        stage_kernel, (), small, "stage", far_in=small, scratch=[dma((len(small),))], limit=1
    )
    (pay,) = call(functools.partial(pay_kernel, halo), (nl, partner), [((2 * block, d), BF16)], "pay", limit=1)
    around = range(n_patches)
    x_rows = lax.ppermute(pay, "wide", [(i, i ^ 1) for i in around])
    y_rows = lax.ppermute(
        pay, "wide", [(i, (i - 1 if i % 2 == 0 else i + 1) % n_patches) for i in around]
    )
    (known,) = call(
        functools.partial(pair_kernel, halo), (pay, x_rows), [((4 * COARSE_DEV, d), BF16)], "pair", limit=1
    )
    have = 2
    while True:
        pieces = [known]
        for k in range(1, min(4, n_patches // have)):
            pieces.append(lax.ppermute(known, "wide", [(i, i ^ (k * have)) for i in around]))
        have *= len(pieces)
        if have == n_patches:
            break
        (known,) = call(
            join_kernel, pieces, [((len(pieces) * known.shape[0], d), BF16)], "join", limit=2
        )
    coarse_rows = len(pieces) * known.shape[0]

    table_a = -(-2 * nodes // LANES) * LANES
    table_b = nodes + 4 * block
    square = ((d, d), BF16)
    base_f, base_c, oh2, sel, inc_f, inc_c, nu, w_send, w_out, u_mess, u_out = call(
        functools.partial(local_kernel, nodes, halo, n_patches),
        (nl, fs, fr, cs, cr, e_bias, n_bias),
        [
            ((edges, d), F32),
            ((coarse_count, d), F32),
            ((edges, table_b), BF16),
            ((coarse_count, coarse_rows), BF16),
            ((nodes, edges), BF16),
            ((TAIL, coarse_count), BF16),
            ((nodes, d), F32),
            square, square, square, square,
        ],
        "local",
        far_in=(fine_edges, coarse_edges, edge_weight_in, edge_weight_out, node_weight_in, node_weight_out),
        scratch=[
            pltpu.VMEM((table_a, d), BF16),
            pltpu.VMEM((edges, d), BF16),
            pltpu.VMEM((coarse_count, d), BF16),
            pltpu.VMEM((d, d), BF16),
            pltpu.VMEM((d, d), BF16),
            pltpu.VMEM((d, d), BF16),
            dma((12,)),
        ],
        limit=16,
    )
    out_f, head = call(
        fine_kernel,
        (partner, x_rows, y_rows, nl, base_f, oh2, inc_f, nu, w_send, w_out, u_mess, u_out,
         e_gain, e_shift, n_gain, n_shift),
        [((nodes, d), BF16), ((TAIL, d), F32)],
        "fine",
        scratch=[pltpu.VMEM((table_b, d), BF16)],
        limit=16,
    )
    (out,) = call(
        functools.partial(coarse_kernel, len(pieces)),
        (out_f, head, nl, nu, base_c, sel, inc_c, w_send, w_out, u_mess, u_out,
         e_gain, e_shift, n_gain, n_shift, *pieces),
        [((nodes, d), BF16)],
        "coarse",
        scratch=[pltpu.VMEM((coarse_rows, d), BF16)],
        limit=8,
        far_out=True,
    )
    return out


def solution(mesh):
    axes = ("grp", "wide", "narrow")
    matrix, vector, whole = P(axes, None), P(axes), P()
    return jax.shard_map(
        shards,
        mesh=mesh,
        in_specs=(matrix, matrix, vector, vector, matrix, vector, vector) + (whole,) * 10,
        out_specs=matrix,
        check_vma=False,
    )
```

time: 29.9 us -> 22.2 us (0.74)
  local copies, waits for them, and re-layouts: 5.13 us -> 0 us
  Pallas kernels: 13.2 us -> 10.3 us
    concatenate x1 -> x0, local copies, waits for them, and re-layouts: 3.04 us -> none  [shards(): known = jnp.concatenate(parts, axis=0)]
    pallas_call x2 -> x6, Pallas kernels: 13.2 us -> 10.3 us  [call(): pl.pallas_call(kernel, out_shape=tuple((kind(*o) for o in outs)), in_spec...]
    slice x5 -> x0, local copies, waits for them, and re-layouts: 1.47 us -> none  [the longest x1 0.75 us: shards(): node_latent[nodes - halo:]]
    unnamed x6 -> x0, local copies, waits for them, and re-layouts: 0.62 us -> none
  transfers between devices with their start and end apart: 6 -> 6, of which waited for: 0 -> 1; matrix products, arithmetic and copies ran while one was open for 15% -> 0% of each run, Pallas kernels for 18% -> 38%
where the time goes in v2:
time: 22.2 us; the launch traced here: 22 us
  starting transfers between devices  11.4 us (51%)
  Pallas kernels  10.3 us (46%)
    pallas_call x6, Pallas kernels, call(): pl.pallas_call(kernel, out_shape=tuple((kind(*o) for o in outs)), in_spec...  10.3 us
    ppermute x3, starting transfers between devices, shards(): lax.ppermute(known, 'wide', [(i, i ^ k * have) for i in around])  4.45 us
    ppermute x1, starting transfers between devices, shards(): lax.ppermute(pay, 'wide', [(i, (i - 1 if i % 2 == 0 else i + 1) % n_patch...  3.57 us
    ppermute x1, starting transfers between devices, shards(): x_rows = lax.ppermute(pay, 'wide', [(i, i ^ 1) for i in around])  2.91 us
    ppermute x1, starting transfers between devices, shards(): partner = lax.ppermute(node_latent, 'narrow', [(0, 1), (1, 0)])  0.49 us
  transfers between devices with their start and end apart: 6, of which 1 were waited for; matrix products, arithmetic and copies ran while one was open for 0% of the time, Pallas kernels for 38%

profile of v2, /device:TPU:0, one launch (start us, length us, event | category | flops | bytes accessed | tf_op | source)
XLA Modules:
  0.0 22.0 jit_solution(1567134540082425147)
XLA Ops:
  0.0 0.5 %collective-permute-start = (bf16[160,512]{1,0:T(8,128)(2,1)}, bf16[160,512]{1,0:T(8,128)(2,1)S(1)}, u32[]{:S(2)}, u32[]{:S(2)}) collective-permute-start(bf16[160,512]{1,0:T(8,128)(2,1)} %refs_0_.1), channel_id=1, source_target_pairs={{0,1},{1,0},{2,3},{3,2},{4,5},{5,4},{6,7},{7,6},{8,9},{9,8},{10,11... | collective-permute-start | bytes 491528 | tf_op jit(solution)/shard_map/ppermute | solution.py:259
  0.5 1.0 %stage.1 = (bf16[160,512]{1,0:T(8,128)(2,1)S(1)}, s32[1,960]{1,0:T(1,128)S(1)}, s32[1,960]{1,0:T(1,128)S(1)}, s32[1,32]{1,0:T(1,128)S(1)}, s32[1,32]{1,0:T(1,128...) custom-call(bf16[160,512]{1,0:T(8,128)(2,1)} %refs_0_.1, ...), custom_call_target="tpu_custom_call" | custom-call | tf_op jit(solution)/shard_map/stage/pallas_call | solution.py:228
  1.5 0.2 collective-permute-done.partner
  1.7 2.9 %collective-permute-start.1 = (bf16[48,512]{1,0:T(8,128)(2,1)S(1)}, bf16[48,512]{1,0:T(8,128)(2,1)S(1)}, u32[]{:S(2)}, u32[]{:S(2)}) collective-permute-start(bf16[48,512]{1,0:T(8,128)(2,1)S(1)} %pay.1), channel_id=1, source_target_pairs={{0,2},{2,0},{4,6},{6,4},{8,10},{10,8},{12,14},{14,12},{1,3},{3,1},... | collective-permute-start | bytes 147464 | tf_op jit(solution)/shard_map/ppermute | solution.py:265
  4.7 3.6 %collective-permute-start.2 = (bf16[48,512]{1,0:T(8,128)(2,1)S(1)}, bf16[48,512]{1,0:T(8,128)(2,1)S(1)}, u32[]{:S(2)}, u32[]{:S(2)}) collective-permute-start(bf16[48,512]{1,0:T(8,128)(2,1)S(1)} %pay.1), channel_id=1, source_target_pairs={{0,14},{2,4},{4,2},{6,8},{8,6},{10,12},{12,10},{14,0},{1,15},{3,5}... | collective-permute-start | bytes 147464 | tf_op jit(solution)/shard_map/ppermute | solution.py:266
  8.2 0.0 collective-permute-done.1.x_rows
  8.2 0.7 %collective-permute-start.3 = (bf16[16,512]{1,0:T(8,128)(2,1)S(1)}, bf16[16,512]{1,0:T(8,128)(2,1)S(1)}, u32[]{:S(2)}, u32[]{:S(2)}) collective-permute-start(bf16[16,512]{1,0:T(8,128)(2,1)S(1)} %pair.1.rest_0_), channel_id=1, source_target_pairs={{0,4},{2,6},{4,0},{6,2},{8,12},{10,14},{12,8},{14,10},{1,5},{3,7},... | collective-permute-start | bytes 49160 | tf_op jit(solution)/shard_map/ppermute | solution.py:276
  8.9 2.6 %collective-permute-start.4 = (bf16[16,512]{1,0:T(8,128)(2,1)S(1)}, bf16[16,512]{1,0:T(8,128)(2,1)S(1)}, u32[]{:S(2)}, u32[]{:S(2)}) collective-permute-start(bf16[16,512]{1,0:T(8,128)(2,1)S(1)} %pair.1.rest_0_), channel_id=1, source_target_pairs={{0,8},{2,10},{4,12},{6,14},{8,0},{10,2},{12,4},{14,6},{1,9},{3,11}... | collective-permute-start | bytes 49160 | tf_op jit(solution)/shard_map/ppermute | solution.py:276
  11.5 1.2 %collective-permute-start.5 = (bf16[16,512]{1,0:T(8,128)(2,1)S(1)}, bf16[16,512]{1,0:T(8,128)(2,1)S(1)}, u32[]{:S(2)}, u32[]{:S(2)}) collective-permute-start(bf16[16,512]{1,0:T(8,128)(2,1)S(1)} %pair.1.rest_0_), channel_id=1, source_target_pairs={{0,12},{2,14},{4,8},{6,10},{8,4},{10,6},{12,0},{14,2},{1,13},{3,15... | collective-permute-start | bytes 49160 | tf_op jit(solution)/shard_map/ppermute | solution.py:276
  12.7 3.9 %local.1 = (f32[960,512]{1,0:T(8,128)S(1)}, f32[32,512]{1,0:T(8,128)S(1)}, bf16[960,256]{1,0:T(8,128)(2,1)S(1)}, bf16[32,64]{1,0:T(8,128)(2,1)S(1)}, bf16[160,96...) custom-call(bf16[160,512]{1,0:T(8,128)(2,1)S(1)} %get-tuple-element., ...), custom_call_target="tpu_custom_call" | custom-call | tf_op jit(solution)/shard_map/local/pallas_call | solution.py:228
  16.6 0.0 collective-permute-done.2.y_rows
  16.6 3.4 %fine.1 = (bf16[160,512]{1,0:T(8,128)(2,1)S(1)}, f32[16,512]{1,0:T(8,128)S(1)}) custom-call(bf16[160,512]{1,0:T(8,128)(2,1)S(1)} %collective-permute-done.partner, bf16[48,512]{1,0:T(8,128)(2,1)S(1)} %collective-permute-done.1.x_rows, bf16[48,512]{1,0:T(8,128)(2,1)S(1)} %collective-permute-done.2.y_rows, bf16[160,512]{1,0:T(8,128)(2,1)S(1)} %get-tuple-element.29.nl, ...), custom_call_target="tpu_custom_call" | custom-call | tf_op jit(solution)/shard_map/fine/pallas_call | solution.py:228
  20.1 0.0 collective-permute-done.3.rest_1_
  20.1 0.0 collective-permute-done.4.rest_2_
  20.1 0.0 collective-permute-done.5.rest_3_
  20.1 1.9 %coarse.1 = bf16[160,512]{1,0:T(8,128)(2,1)} custom-call(bf16[160,512]{1,0:T(8,128)(2,1)S(1)} %get-tuple-element.48.out_f, f32[16,512]{1,0:T(8,128)S(1)} %get-tuple-element.49.head, bf16[160,512]{1,0:T(8,128)(2,1)S(1)} %get-tuple-element.29.nl, f32[160,512]{1,0:T(8,128)S(1)} %get-tuple-element.39.nu, f32[32,512]{1,0:T(8,128)S(1)} %get-tuple-element.50.base_c, ...), custom_call_target="tpu_custom_call" | custom-call | tf_op jit(solution)/shard_map/coarse/pallas_call | solution.py:228
  (2 shorter events, 0.0 us)
Async XLA Ops:
  0.0 1.7 %collective-permute-start = (bf16[160,512]{1,0:T(8,128)(2,1)}, bf16[160,512]{1,0:T(8,128)(2,1)S(1)}, u32[]{:S(2)}, u32[]{:S(2)}) collective-permute-start(bf16[160,512]{1,0:T(8,128)(2,1)} %refs_0_.1), channel_id=1, source_target_pairs={{0,1},{1,0},{2,3},{3,2},{4,5},{5,4},{6,7},{7,6},{8,9},{9,8},{10,11... | collective-permute-start | bytes 491528 | tf_op jit(solution)/shard_map/ppermute | solution.py:259
  1.7 6.5 %collective-permute-start.1 = (bf16[48,512]{1,0:T(8,128)(2,1)S(1)}, bf16[48,512]{1,0:T(8,128)(2,1)S(1)}, u32[]{:S(2)}, u32[]{:S(2)}) collective-permute-start(bf16[48,512]{1,0:T(8,128)(2,1)S(1)} %pay.1), channel_id=1, source_target_pairs={{0,2},{2,0},{4,6},{6,4},{8,10},{10,8},{12,14},{14,12},{1,3},{3,1},... | collective-permute-start | bytes 147464 | tf_op jit(solution)/shard_map/ppermute | solution.py:265
  4.7 11.9 %collective-permute-start.2 = (bf16[48,512]{1,0:T(8,128)(2,1)S(1)}, bf16[48,512]{1,0:T(8,128)(2,1)S(1)}, u32[]{:S(2)}, u32[]{:S(2)}) collective-permute-start(bf16[48,512]{1,0:T(8,128)(2,1)S(1)} %pay.1), channel_id=1, source_target_pairs={{0,14},{2,4},{4,2},{6,8},{8,6},{10,12},{12,10},{14,0},{1,15},{3,5}... | collective-permute-start | bytes 147464 | tf_op jit(solution)/shard_map/ppermute | solution.py:266
  8.2 11.8 %collective-permute-start.3 = (bf16[16,512]{1,0:T(8,128)(2,1)S(1)}, bf16[16,512]{1,0:T(8,128)(2,1)S(1)}, u32[]{:S(2)}, u32[]{:S(2)}) collective-permute-start(bf16[16,512]{1,0:T(8,128)(2,1)S(1)} %pair.1.rest_0_), channel_id=1, source_target_pairs={{0,4},{2,6},{4,0},{6,2},{8,12},{10,14},{12,8},{14,10},{1,5},{3,7},... | collective-permute-start | bytes 49160 | tf_op jit(solution)/shard_map/ppermute | solution.py:276
  8.9 11.2 %collective-permute-start.4 = (bf16[16,512]{1,0:T(8,128)(2,1)S(1)}, bf16[16,512]{1,0:T(8,128)(2,1)S(1)}, u32[]{:S(2)}, u32[]{:S(2)}) collective-permute-start(bf16[16,512]{1,0:T(8,128)(2,1)S(1)} %pair.1.rest_0_), channel_id=1, source_target_pairs={{0,8},{2,10},{4,12},{6,14},{8,0},{10,2},{12,4},{14,6},{1,9},{3,11}... | collective-permute-start | bytes 49160 | tf_op jit(solution)/shard_map/ppermute | solution.py:276
  11.5 8.6 %collective-permute-start.5 = (bf16[16,512]{1,0:T(8,128)(2,1)S(1)}, bf16[16,512]{1,0:T(8,128)(2,1)S(1)}, u32[]{:S(2)}, u32[]{:S(2)}) collective-permute-start(bf16[16,512]{1,0:T(8,128)(2,1)S(1)} %pair.1.rest_0_), channel_id=1, source_target_pairs={{0,12},{2,14},{4,8},{6,10},{8,4},{10,6},{12,0},{14,2},{1,13},{3,15... | collective-permute-start | bytes 49160 | tf_op jit(solution)/shard_map/ppermute | solution.py:276

commit v3 on v2

v3 whole, which is shorter than its diff:
```python
import functools

import jax
import jax.numpy as jnp
from jax import lax
from jax.experimental import pallas as pl
from jax.experimental.pallas import tpu as pltpu
from jax.sharding import PartitionSpec as P


COARSE_DEV = 4
LANES = 128
CHUNKS = 3
BF16 = jnp.bfloat16
F32 = jnp.float32
MIB = 1 << 20


def silu_of_half(u):
    return u + u * jnp.tanh(u)


def normalized(values):
    center = values - jnp.mean(values, axis=-1, keepdims=True)
    spread = jnp.mean(center * center, axis=-1, keepdims=True)
    return center * lax.rsqrt(spread + 1e-05)


def dot(a, b):
    return jnp.dot(a, b, preferred_element_type=F32)


def columns(row):
    return jnp.broadcast_to(row, (LANES, row.shape[1])).T


def one_hot(cols, width, value=1.0):
    lane = lax.broadcasted_iota(jnp.int32, cols[0].shape, 1)
    blocks = []
    for b in range(width // LANES):
        hit = cols[0] == lane + b * LANES
        for c in cols[1:]:
            hit = hit | (c == lane + b * LANES)
        blocks.append(jnp.where(hit, value, 0.0).astype(BF16))
    return jnp.concatenate(blocks, axis=1)


def stage_kernel(n, *refs):
    sems = refs[-1]
    copies = [pltpu.make_async_copy(refs[k], refs[k - n - 1], sems.at[k]) for k in range(n)]
    for c in copies:
        c.start()
    for c in copies:
        c.wait()


def pay_kernel(halo, nl, partner, pay):
    nodes = nl.shape[0]
    pay[...] = jnp.concatenate(
        [nl[nodes - halo :, :], nl[:COARSE_DEV, :], partner[nodes - halo :, :], partner[:COARSE_DEV, :]],
        axis=0,
    )


def pair_kernel(halo, pay, x_rows, _, known, rich):
    block = halo + COARSE_DEV
    pair = jnp.concatenate(
        [r[s : s + COARSE_DEV, :] for r in (pay, x_rows) for s in (halo, block + halo)], axis=0
    )
    known[...] = pair
    rich[: pair.shape[0], :] = pair
    rich[pair.shape[0] :, :] = x_rows[...]


def join_kernel(*refs):
    at = 0
    for r in refs[:-1]:
        refs[-1][at : at + r.shape[0], :] = r[...]
        at += r.shape[0]


def places(n_patches):
    wide = lax.axis_index("wide")
    half = lax.axis_index("narrow")
    y_patch = jnp.where(wide % 2 == 0, wide + n_patches - 1, wide + 1) % n_patches
    return wide, half, wide * 2 + half, y_patch


def local_kernel(
    nodes, halo, n_patches,
    nl, fs, fr, cs, cr, e_bias, n_bias, e_shift, ce, w_in, u_in,
    base_c, oh1, oh2, sel, inc, shifts, nu, table,
):
    d = nl.shape[1]
    wide, half, device, y_patch = places(n_patches)
    patch = 2 * nodes
    first = nodes - halo
    block = halo + COARSE_DEV

    recv = fr[...] - device * nodes
    send = fs[...]

    def offset(p):
        off = send - p * patch
        inside = (off >= 0) & (off < patch)
        upper = (off >= nodes).astype(jnp.int32)
        return inside, upper, off - upper * nodes

    inside, upper, loc = offset(wide)
    own = jnp.where(inside & (upper == half), loc + nodes, -1)
    pos = jnp.where(inside & (upper != half), loc, -1)
    for k, p in enumerate((wide ^ 1, y_patch)):
        inside, upper, loc = offset(p)
        slot = jnp.where(upper == half, 0, 1)
        at = nodes + k * 2 * block + slot * block + loc - first
        pos = jnp.where(inside, at, pos)

    recv_c = cr[...] - device * nodes
    chip_rows = cs[...].astype(F32)
    owner = jnp.floor((chip_rows + 0.5) * (1.0 / nodes)).astype(jnp.int32)
    slot_c = cs[...] - owner * nodes
    pos_c = ((owner // 2) ^ wide) * (2 * COARSE_DEV) + ((owner % 2) ^ half) * COARSE_DEV + slot_c

    total = fr.shape[1] + cr.shape[1]
    spare = jnp.full((1, inc.shape[1] - total), -1, jnp.int32)
    recv_all = jnp.concatenate([recv, recv_c, spare], axis=1)
    node_at = lax.broadcasted_iota(jnp.int32, inc.shape, 0)
    marks = jnp.where(node_at == recv_all, 1.0, 0.0)
    inc[...] = marks.astype(BF16)
    shifts[...] = jnp.sum(marks, axis=1, keepdims=True) * e_shift[...]
    wide_c = -(-sel.shape[1] // LANES) * LANES
    sel[...] = one_hot((columns(pos_c),), wide_c)[:, : sel.shape[1]]
    oh_c = one_hot((columns(recv_c),), table.shape[0])
    oh1[...] = one_hot((columns(recv), columns(own)), oh1.shape[1], 0.5)
    oh2[...] = one_hot((columns(pos),), oh2.shape[1], 0.5)
    table[2 * nodes :, :] = jnp.zeros_like(table[2 * nodes :, :])

    node_rows = nl[...]
    table[0:nodes, :] = dot(node_rows, w_in[2 * d :, :]).astype(BF16)
    table[nodes : 2 * nodes, :] = dot(node_rows, w_in[d : 2 * d, :]).astype(BF16)
    nu[...] = 0.5 * (dot(node_rows, u_in[:d, :]) + n_bias[...])
    base_c[...] = 0.5 * (dot(ce[...], w_in[:d, :]) + dot(oh_c, table[...]) + e_bias[...])


def base_kernel(oh1, table, w_in, e_bias, fe, base_f):
    rows, d = fe.shape
    step = rows // 2
    for k in range(2):
        s = slice(k * step, (k + 1) * step)
        own = 0.5 * (dot(fe[s, :], w_in[:d, :]) + e_bias[...])
        base_f[s, :] = own + dot(oh1[s, :], table[...])


def w_send(w_in):
    d = w_in.shape[1]
    return w_in[d : 2 * d, :]


def main_kernel(
    n_patches, y_choices, n_pieces,
    partner, x_rows, nl, base_f, base_c, oh2, sel, inc, shifts, nu, w_in, w_out, u_in, u_out,
    e_gain, n_gain, n_shift, *refs,
):
    y_refs, refs = refs[: len(y_choices)], refs[len(y_choices) :]
    pieces, (out, table, picks, hidden, mess) = refs[:n_pieces], refs[n_pieces:]
    a = partner.shape[0]
    b = a + x_rows.shape[0]
    n_rows = x_rows.shape[0]
    y_rows = y_refs[0][y_refs[0].shape[0] - n_rows :, :]
    if len(y_choices) > 1:
        wide, _, _, y_patch = places(n_patches)
        pair_step = (wide // 2) ^ (y_patch // 2)
        for k, ref in zip(y_choices[1:], y_refs[1:]):
            y_rows = jnp.where(pair_step == k, ref[ref.shape[0] - n_rows :, :], y_rows)
    size = picks.shape[0] // n_pieces
    for k, r in enumerate(pieces):
        picks[k * size : (k + 1) * size, :] = r[:size, :]
    table[0:a, :] = partner[...]
    table[a:b, :] = x_rows[...]
    table[b:, :] = y_rows
    w_s = w_send(w_in)
    table[...] = dot(table[...], w_s).astype(BF16)

    rows, coarse = base_f.shape[0], base_c.shape[0]
    step = rows // CHUNKS
    parts = [slice(k * step, (k + 1) * step) for k in range(CHUNKS)] + [slice(rows, rows + coarse)]

    def first(k):
        s = parts[k]
        if k < CHUNKS:
            half = base_f[s, :] + dot(oh2[s, :], table[...])
        else:
            picked = dot(sel[...], picks[...]).astype(BF16)
            half = base_c[...] + 0.5 * dot(picked, w_s)
        hidden[s, :] = silu_of_half(half).astype(BF16)

    def second(k):
        s = parts[k]
        mess[s, :] = normalized(dot(hidden[s, :], w_out[...])).astype(BF16)

    mess[rows + coarse :, :] = jnp.zeros_like(mess[rows + coarse :, :])
    order = [CHUNKS] + list(range(CHUNKS))
    first(order[0])
    for now, then in zip(order, order[1:]):
        first(then)
        second(now)
    second(order[-1])
    summed = dot(inc[...], mess[...]) * e_gain[...] + shifts[...]
    d = nl.shape[1]
    half = nu[...] + 0.5 * dot(summed.astype(BF16), u_in[d:, :])
    update = normalized(dot(silu_of_half(half).astype(BF16), u_out[...]))
    out[...] = (nl[...].astype(F32) + (update * n_gain[...] + n_shift[...])).astype(BF16)


NEAR = pl.BlockSpec(memory_space=pltpu.VMEM)
FAR = pl.BlockSpec(memory_space=pltpu.HBM)


def near(*arrays):
    return [pltpu.with_memory_space_constraint(a, pltpu.VMEM) for a in arrays]


def call(kernel, near_in, outs, far_in=(), scratch=(), limit=8, far_out=False, cost=None):
    outs = [(o.shape, o.dtype) if hasattr(o, "shape") else o for o in outs]
    kind = (lambda s, t: jax.ShapeDtypeStruct(s, t)) if far_out else (lambda s, t: pltpu.VMEM(s, t))
    return pl.pallas_call(
        kernel,
        out_shape=tuple(kind(*o) for o in outs),
        in_specs=[NEAR] * len(near_in) + [FAR] * len(far_in),
        out_specs=tuple([NEAR] * len(outs)),
        scratch_shapes=list(scratch),
        compiler_params=pltpu.CompilerParams(vmem_limit_bytes=limit * MIB),
        cost_estimate=pl.CostEstimate(flops=cost or 0, bytes_accessed=cost or 0, transcendentals=0),
    )(*near(*near_in), *[pltpu.with_memory_space_constraint(a, pltpu.HBM) for a in far_in])


def shards(
    node_latent, fine_edges, fine_senders, fine_receivers, coarse_edges, coarse_senders,
    coarse_receivers, edge_weight_in, edge_bias, edge_weight_out, edge_gain, edge_shift,
    node_weight_in, node_bias, node_weight_out, node_gain, node_shift,
):
    nodes, d = node_latent.shape
    halo = nodes // 8
    block = halo + COARSE_DEV
    n_patches = lax.axis_size("wide")
    edges, coarse_count = fine_edges.shape[0], coarse_edges.shape[0]
    small = [node_latent] + [
        v.reshape(1, -1)
        for v in (
            fine_senders, fine_receivers, coarse_senders, coarse_receivers, edge_bias, node_bias,
            edge_gain, edge_shift, node_gain, node_shift,
        )
    ]
    dma = pltpu.SemaphoreType.DMA

    partner = lax.ppermute(node_latent, "narrow", [(0, 1), (1, 0)])
    nl, fs, fr, cs, cr, e_bias, n_bias, e_gain, e_shift, n_gain, n_shift = call(
        functools.partial(stage_kernel, len(small)), (), small,
        far_in=small + [fine_edges, edge_weight_in, node_weight_in], scratch=[dma((len(small),))], limit=1
    )
    (pay,) = call(functools.partial(pay_kernel, halo), (nl, partner), [((2 * block, d), BF16)], limit=1)
    around = range(n_patches)
    x_rows = lax.ppermute(pay, "wide", [(i, i ^ 1) for i in around])
    table_a = -(-2 * nodes // LANES) * LANES
    table_b = nodes + 4 * block
    padded = -(-(edges + coarse_count) // LANES) * LANES
    base_c, oh1, oh2, sel, inc, shifts, nu, table = call(
        functools.partial(local_kernel, nodes, halo, n_patches),
        (nl, fs, fr, cs, cr, e_bias, n_bias, e_shift, coarse_edges, edge_weight_in, node_weight_in),
        [
            ((coarse_count, d), F32),
            ((edges, table_a), BF16),
            ((edges, table_b), BF16),
            ((coarse_count, 2 * n_patches * COARSE_DEV), BF16),
            ((nodes, padded), BF16),
            ((nodes, d), F32),
            ((nodes, d), F32),
            ((table_a, d), BF16),
        ],
        limit=16,
    )
    known, rich = call(
        functools.partial(pair_kernel, halo), (pay, x_rows, base_c),
        [((4 * COARSE_DEV, d), BF16), ((4 * COARSE_DEV + 2 * block, d), BF16)], limit=1,
    )
    shift = lambda v, k: lax.ppermute(v, "wide", [(i, i ^ k) for i in around])
    near_ring = n_patches == 8
    if near_ring:
        three = shift(rich, 6)
        two = shift(known, 4)
        one = shift(rich, 2)
        pieces = [known, one, two, three]
        y_choices, y_refs = (1, 3), (one, three)
    else:
        y_choices = (0,)
        y_refs = (
            lax.ppermute(
                pay, "wide", [(i, (i - 1 if i % 2 == 0 else i + 1) % n_patches) for i in around]
            ),
        )
        have = 2
        while True:
            pieces = [known]
            for k in range(1, min(4, n_patches // have)):
                pieces.append(shift(known, k * have))
            have *= len(pieces)
            if have == n_patches:
                break
            (known,) = call(
                join_kernel, pieces, [((len(pieces) * known.shape[0], d), BF16)], limit=2
            )
    coarse_rows = len(pieces) * known.shape[0]

    (base_f,) = call(
        base_kernel, (oh1, table, edge_weight_in, e_bias, fine_edges), [((edges, d), F32)], limit=16
    )
    (out,) = call(
        functools.partial(main_kernel, n_patches, y_choices, len(pieces)),
        (partner, x_rows, nl, base_f, base_c, oh2, sel, inc, shifts, nu,
         edge_weight_in, edge_weight_out, node_weight_in, node_weight_out,
         e_gain, n_gain, n_shift, *y_refs, *pieces),
        [((nodes, d), BF16)],
        scratch=[
            pltpu.VMEM((table_b, d), BF16),
            pltpu.VMEM((coarse_rows, d), BF16),
            pltpu.VMEM((padded, d), BF16),
            pltpu.VMEM((padded, d), BF16),
        ],
        limit=16,
        far_out=True,
    )
    return out


def solution(mesh):
    axes = ("grp", "wide", "narrow")
    matrix, vector, whole = P(axes, None), P(axes), P()
    return jax.shard_map(
        shards,
        mesh=mesh,
        in_specs=(matrix, matrix, vector, vector, matrix, vector, vector) + (whole,) * 10,
        out_specs=matrix,
        check_vma=False,
    )
```

time: 22.2 us -> 19.3 us (0.87)
  waiting for transfers between devices: 0.22 us -> 4.52 us
  Pallas kernels: 10.3 us -> 6.42 us
  starting transfers between devices: 11.4 us -> 8.16 us
    pallas_call x6, Pallas kernels: 10.3 us -> 6.42 us  [call(): pl.pallas_call(kernel, out_shape=tuple((kind(*o) for o in outs)), in_spec...]
    ppermute x4 -> x3, waiting for transfers between devices: 0.01 us -> 3.31 us  [shards(): shift = lambda v, k: lax.ppermute(v, 'wide', [(i, i ^ k) for i in around])]
    ppermute x4 -> x3, starting transfers between devices: 8.02 us -> 4.76 us  [shards(): shift = lambda v, k: lax.ppermute(v, 'wide', [(i, i ^ k) for i in around])]
    ppermute x1, waiting for transfers between devices: 0.01 us -> 1.18 us  [shards(): x_rows = lax.ppermute(pay, 'wide', [(i, i ^ 1) for i in around])]
  transfers between devices with their start and end apart: 6 -> 5, of which waited for: 1 -> 2; matrix products, arithmetic and copies ran while one was open for 0% -> 0% of each run, Pallas kernels for 38% -> 17%
where the time goes in v3:
time: 19.3 us; the launch traced here: 19.2 us
  starting transfers between devices  8.16 us (42%)
  Pallas kernels  6.42 us (33%)
  waiting for transfers between devices  4.52 us (23%)
    pallas_call x6, Pallas kernels, call(): pl.pallas_call(kernel, out_shape=tuple((kind(*o) for o in outs)), in_spec...  6.42 us
    ppermute x3, starting transfers between devices, shards(): shift = lambda v, k: lax.ppermute(v, 'wide', [(i, i ^ k) for i in around])  4.76 us
    ppermute x3, waiting for transfers between devices, shards(): shift = lambda v, k: lax.ppermute(v, 'wide', [(i, i ^ k) for i in around])  3.31 us
    ppermute x1, starting transfers between devices, shards(): x_rows = lax.ppermute(pay, 'wide', [(i, i ^ 1) for i in around])  2.91 us
    ppermute x1, waiting for transfers between devices, shards(): x_rows = lax.ppermute(pay, 'wide', [(i, i ^ 1) for i in around])  1.18 us
    ppermute x1, starting transfers between devices, shards(): partner = lax.ppermute(node_latent, 'narrow', [(0, 1), (1, 0)])  0.49 us
  transfers between devices with their start and end apart: 5, of which 2 were waited for; matrix products, arithmetic and copies ran while one was open for 0% of the time, Pallas kernels for 17%

profile of v3, /device:TPU:0, one launch (start us, length us, event | category | flops | bytes accessed | tf_op | source)
XLA Modules:
  0.0 19.2 jit_solution(1328042836297315871)
XLA Ops:
  0.0 0.5 %collective-permute-start = (bf16[160,512]{1,0:T(8,128)(2,1)}, bf16[160,512]{1,0:T(8,128)(2,1)S(1)}, u32[]{:S(2)}, u32[]{:S(2)}) collective-permute-start(bf16[160,512]{1,0:T(8,128)(2,1)} %refs_0_.1), channel_id=1, source_target_pairs={{0,1},{1,0},{2,3},{3,2},{4,5},{5,4},{6,7},{7,6},{8,9},{9,8},{10,11... | collective-permute-start | bytes 491528 | tf_op jit(solution)/shard_map/ppermute | solution.py:256
  0.5 0.0 copy-start
  0.5 0.0 copy-start.1
  0.5 0.0 copy-start.5
  0.5 1.2 %shard_map.163 = (bf16[160,512]{1,0:T(8,128)(2,1)S(1)}, s32[1,960]{1,0:T(1,128)S(1)}, s32[1,960]{1,0:T(1,128)S(1)}, s32[1,32]{1,0:T(1,128)S(1)}, s32[1,32]{1,0:T...) custom-call(bf16[160,512]{1,0:T(8,128)(2,1)} %refs_0_.1, ...), custom_call_target="tpu_custom_call" | custom-call | tf_op jit(solution)/shard_map/pallas_call | solution.py:226
  1.7 0.0 copy-start.2
  1.7 0.0 collective-permute-done.partner
  1.7 2.9 %collective-permute-start.1 = (bf16[48,512]{1,0:T(8,128)(2,1)S(1)}, bf16[48,512]{1,0:T(8,128)(2,1)S(1)}, u32[]{:S(2)}, u32[]{:S(2)}) collective-permute-start(bf16[48,512]{1,0:T(8,128)(2,1)S(1)} %shard_map.164.pay), channel_id=1, source_target_pairs={{0,2},{2,0},{4,6},{6,4},{8,10},{10,8},{12,14},{14,12},{1,3},{3,1},... | collective-permute-start | bytes 147464 | tf_op jit(solution)/shard_map/ppermute | solution.py:263
  4.7 0.0 copy-done
  4.7 0.0 copy-done.1
  4.7 0.0 copy-done.5
  4.7 0.9 %shard_map.165 = (f32[32,512]{1,0:T(8,128)S(1)}, bf16[960,384]{1,0:T(8,128)(2,1)S(1)}, bf16[960,256]{1,0:T(8,128)(2,1)S(1)}, bf16[32,64]{1,0:T(8,128)(2,1)S(1)},...) custom-call(bf16[160,512]{1,0:T(8,128)(2,1)S(1)} %get-tuple-element., ...), custom_call_target="tpu_custom_call" | custom-call | tf_op jit(solution)/shard_map/pallas_call | solution.py:226
  5.5 1.2 %collective-permute-done.1.x_rows = bf16[48,512]{1,0:T(8,128)(2,1)S(1)} collective-permute-done((bf16[48,512]{1,0:T(8,128)(2,1)S(1)}, bf16[48,512]{1,0:T(8,128)(2,1)S(1)}, u32[]{:S(2)}, u32[]{:S(2)}) %collective-permute-start.1) | collective-permute-done | bytes 49184 | tf_op jit(solution)/shard_map/ppermute | solution.py:263
  6.7 2.2 %collective-permute-start.2 = (bf16[64,512]{1,0:T(8,128)(2,1)S(1)}, bf16[64,512]{1,0:T(8,128)(2,1)S(1)}, u32[]{:S(2)}, u32[]{:S(2)}) collective-permute-start(bf16[64,512]{1,0:T(8,128)(2,1)S(1)} %get-tuple-element.45), channel_id=1, source_target_pairs={{0,4},{2,6},{4,0},{6,2},{8,12},{10,14},{12,8},{14,10},{1,5},{3,7},... | collective-permute-start | bytes 196616 | tf_op jit(solution)/shard_map/ppermute | solution.py:286
  8.9 2.5 %collective-permute-start.3 = (bf16[64,512]{1,0:T(8,128)(2,1)S(1)}, bf16[64,512]{1,0:T(8,128)(2,1)S(1)}, u32[]{:S(2)}, u32[]{:S(2)}) collective-permute-start(bf16[64,512]{1,0:T(8,128)(2,1)S(1)} %get-tuple-element.45), channel_id=1, source_target_pairs={{0,12},{2,14},{4,8},{6,10},{8,4},{10,6},{12,0},{14,2},{1,13},{3,15... | collective-permute-start | bytes 196616 | tf_op jit(solution)/shard_map/ppermute | solution.py:286
  11.4 0.1 collective-permute-start.4
  11.5 0.0 copy-done.2
  11.5 1.2 %shard_map.166.base_f = f32[960,512]{1,0:T(8,128)S(1)} custom-call(bf16[960,384]{1,0:T(8,128)(2,1)S(1)} %get-tuple-element.34.oh1, bf16[384,512]{1,0:T(8,128)(2,1)S(1)} %get-tuple-element.35.table, bf16[1536,512]{1,0:T(8,128)(2,1)S(1)} %copy-done, f32[1,512]{1,0:T(1,128)S(1)} %get-tuple-element.31.e_bias, bf16[960,512]{1,0:T(8,128)(2,1)S(1)} %copy-done.2), custom_call_target="tpu_custom_call" | custom-call | tf_op jit(solution)/shard_map/pallas_call | solution.py:226
  12.7 3.3 %collective-permute-done.4.refs_4_ = bf16[16,512]{1,0:T(8,128)(2,1)S(1)} collective-permute-done((bf16[16,512]{1,0:T(8,128)(2,1)S(1)}, bf16[16,512]{1,0:T(8,128)(2,1)S(1)}, u32[]{:S(2)}, u32[]{:S(2)}) %collective-permute-start.4) | collective-permute-done | bytes 16416 | tf_op jit(solution)/shard_map/ppermute | solution.py:286
  16.0 0.0 collective-permute-done.2.refs_0_.refs_3_
  16.0 0.0 collective-permute-done.3.refs_1_.refs_5_
  16.0 0.0 copy-done.3
  16.0 0.0 copy-done.4
  16.1 3.1 %shard_map.168 = bf16[160,512]{1,0:T(8,128)(2,1)} custom-call(bf16[160,512]{1,0:T(8,128)(2,1)S(1)} %collective-permute-done.partner, bf16[48,512]{1,0:T(8,128)(2,1)S(1)} %collective-permute-done.1.x_rows, bf16[160,512]{1,0:T(8,128)(2,1)S(1)} %get-tuple-element.26.nl, f32[960,512]{1,0:T(8,128)S(1)} %shard_map.166.base_f, ...), custom_call_target="tpu_custom_call" | custom-call | tf_op jit(solution)/shard_map/pallas_call | solution.py:226
  (4 shorter events, 0.0 us)
Async XLA Ops:
  0.0 1.7 %collective-permute-start = (bf16[160,512]{1,0:T(8,128)(2,1)}, bf16[160,512]{1,0:T(8,128)(2,1)S(1)}, u32[]{:S(2)}, u32[]{:S(2)}) collective-permute-start(bf16[160,512]{1,0:T(8,128)(2,1)} %refs_0_.1), channel_id=1, source_target_pairs={{0,1},{1,0},{2,3},{3,2},{4,5},{5,4},{6,7},{7,6},{8,9},{9,8},{10,11... | collective-permute-start | bytes 491528 | tf_op jit(solution)/shard_map/ppermute | solution.py:256
  0.5 4.2 %copy-start = (bf16[1536,512]{1,0:T(8,128)(2,1)S(1)}, bf16[1536,512]{1,0:T(8,128)(2,1)}, u32[]{:S(2)}) copy-start(bf16[1536,512]{1,0:T(8,128)(2,1)} %w_in.5) | copy-start | bytes 4718596
  0.5 4.2 %copy-start.1 = (bf16[1024,512]{1,0:T(8,128)(2,1)S(1)}, bf16[1024,512]{1,0:T(8,128)(2,1)}, u32[]{:S(2)}) copy-start(bf16[1024,512]{1,0:T(8,128)(2,1)} %u_in.3) | copy-start | bytes 3145732
  0.5 4.2 %copy-start.5 = (bf16[32,512]{1,0:T(8,128)(2,1)S(1)}, bf16[32,512]{1,0:T(8,128)(2,1)}, u32[]{:S(2)}) copy-start(bf16[32,512]{1,0:T(8,128)(2,1)} %ce.1) | copy-start | bytes 98308
  1.7 9.8 %copy-start.2 = (bf16[960,512]{1,0:T(8,128)(2,1)S(1)}, bf16[960,512]{1,0:T(8,128)(2,1)}, u32[]{:S(2)}) copy-start(bf16[960,512]{1,0:T(8,128)(2,1)} %fe.1) | copy-start | bytes 2949124
  1.7 5.0 %collective-permute-start.1 = (bf16[48,512]{1,0:T(8,128)(2,1)S(1)}, bf16[48,512]{1,0:T(8,128)(2,1)S(1)}, u32[]{:S(2)}, u32[]{:S(2)}) collective-permute-start(bf16[48,512]{1,0:T(8,128)(2,1)S(1)} %shard_map.164.pay), channel_id=1, source_target_pairs={{0,2},{2,0},{4,6},{6,4},{8,10},{10,8},{12,14},{14,12},{1,3},{3,1},... | collective-permute-start | bytes 147464 | tf_op jit(solution)/shard_map/ppermute | solution.py:263
  6.7 9.3 %collective-permute-start.2 = (bf16[64,512]{1,0:T(8,128)(2,1)S(1)}, bf16[64,512]{1,0:T(8,128)(2,1)S(1)}, u32[]{:S(2)}, u32[]{:S(2)}) collective-permute-start(bf16[64,512]{1,0:T(8,128)(2,1)S(1)} %get-tuple-element.45), channel_id=1, source_target_pairs={{0,4},{2,6},{4,0},{6,2},{8,12},{10,14},{12,8},{14,10},{1,5},{3,7},... | collective-permute-start | bytes 196616 | tf_op jit(solution)/shard_map/ppermute | solution.py:286
  8.9 7.1 %collective-permute-start.3 = (bf16[64,512]{1,0:T(8,128)(2,1)S(1)}, bf16[64,512]{1,0:T(8,128)(2,1)S(1)}, u32[]{:S(2)}, u32[]{:S(2)}) collective-permute-start(bf16[64,512]{1,0:T(8,128)(2,1)S(1)} %get-tuple-element.45), channel_id=1, source_target_pairs={{0,12},{2,14},{4,8},{6,10},{8,4},{10,6},{12,0},{14,2},{1,13},{3,15... | collective-permute-start | bytes 196616 | tf_op jit(solution)/shard_map/ppermute | solution.py:286
  11.4 4.6 %collective-permute-start.4 = (bf16[16,512]{1,0:T(8,128)(2,1)S(1)}, bf16[16,512]{1,0:T(8,128)(2,1)S(1)}, u32[]{:S(2)}, u32[]{:S(2)}) collective-permute-start(bf16[16,512]{1,0:T(8,128)(2,1)S(1)} %get-tuple-element.46.refs_2_), channel_id=1, source_target_pairs={{0,8},{2,10},{4,12},{6,14},{8,0},{10,2},{12,4},{14,6},{1,9},{3,11}... | collective-permute-start | bytes 49160 | tf_op jit(solution)/shard_map/ppermute | solution.py:286
  11.5 4.5 %copy-start.3 = (bf16[512,512]{1,0:T(8,128)(2,1)S(1)}, bf16[512,512]{1,0:T(8,128)(2,1)}, u32[]{:S(2)}) copy-start(bf16[512,512]{1,0:T(8,128)(2,1)} %w_out.1) | copy-start | bytes 1572868
  11.5 4.5 %copy-start.4 = (bf16[512,512]{1,0:T(8,128)(2,1)S(1)}, bf16[512,512]{1,0:T(8,128)(2,1)}, u32[]{:S(2)}) copy-start(bf16[512,512]{1,0:T(8,128)(2,1)} %u_out.1) | copy-start | bytes 1572868

commit v4 on v3

--- a/solution.py
+++ b/solution.py
@@ -11,6 +11,7 @@
 COARSE_DEV = 4
 LANES = 128
 CHUNKS = 3
+RING = 8
 BF16 = jnp.bfloat16
 F32 = jnp.float32
 MIB = 1 << 20
@@ -56,20 +57,48 @@
 
 def pay_kernel(halo, nl, partner, pay):
     nodes = nl.shape[0]
-    pay[...] = jnp.concatenate(
-        [nl[nodes - halo :, :], nl[:COARSE_DEV, :], partner[nodes - halo :, :], partner[:COARSE_DEV, :]],
-        axis=0,
-    )
+    pick = lambda r: jnp.concatenate([r[nodes - halo :, :], r[:COARSE_DEV, :]], axis=0)
+    own, other = pick(nl), pick(partner)
+    low = lax.axis_index("narrow") == 0
+    pay[...] = jnp.concatenate([jnp.where(low, own, other), jnp.where(low, other, own)], axis=0)
+
+
+def coarse_of(rows, halo):
+    block = halo + COARSE_DEV
+    return [rows[halo:block, :], rows[block + halo : 2 * block, :]]
 
 
 def pair_kernel(halo, pay, x_rows, _, known, rich):
+    known[...] = jnp.concatenate(coarse_of(pay, halo) + coarse_of(x_rows, halo), axis=0)
+    rich[...] = jnp.concatenate([known[...]] + halos_of(x_rows, halo), axis=0)
+
+
+def both_kernel(first, second, _, both):
+    low = lax.axis_index("narrow") == 0
+    n, m = first.shape[0], both.shape[0] - first.shape[0]
+    both[:n, :] = jnp.where(low, first[...], second[...])
+    both[n:, :] = first[:m, :]
+
+
+def halos_of(rows, halo):
     block = halo + COARSE_DEV
-    pair = jnp.concatenate(
-        [r[s : s + COARSE_DEV, :] for r in (pay, x_rows) for s in (halo, block + halo)], axis=0
-    )
-    known[...] = pair
-    rich[: pair.shape[0], :] = pair
-    rich[pair.shape[0] :, :] = x_rows[...]
+    return [rows[:halo, :], rows[block : block + halo, :]]
+
+
+def collect_kernel(halo, x_rows, known, both, other, far, picks):
+    n, m = 2 * halo, known.shape[0]
+    low = lax.axis_index("narrow") == 0
+    even = lax.axis_index("wide") % 2 == 0
+    zero, one = jnp.where(low, both[...], other[...]), jnp.where(low, other[...], both[...])
+    picks[...] = jnp.concatenate([known[...], one[:m], one[m + n :], zero[:m]], axis=0)
+    source = jnp.where(even, zero[m : m + n], one[m : m + n])
+    far[...] = jnp.concatenate([x_rows[...], source, known[: 2 * COARSE_DEV]], axis=0)
+
+
+def wrap_kernel(halo, x_rows, y_rows, far):
+    far[...] = jnp.concatenate(
+        [x_rows[...]] + halos_of(y_rows[...], halo) + [y_rows[: 2 * COARSE_DEV, :]], axis=0
+    )
 
 
 def join_kernel(*refs):
@@ -111,16 +140,20 @@
     pos = jnp.where(inside & (upper != half), loc, -1)
     for k, p in enumerate((wide ^ 1, y_patch)):
         inside, upper, loc = offset(p)
-        slot = jnp.where(upper == half, 0, 1)
-        at = nodes + k * 2 * block + slot * block + loc - first
+        at = nodes + k * 2 * block + upper * (block, halo)[k] + loc - first
         pos = jnp.where(inside, at, pos)
 
     recv_c = cr[...] - device * nodes
     chip_rows = cs[...].astype(F32)
     owner = jnp.floor((chip_rows + 0.5) * (1.0 / nodes)).astype(jnp.int32)
     slot_c = cs[...] - owner * nodes
-    pos_c = ((owner // 2) ^ wide) * (2 * COARSE_DEV) + ((owner % 2) ^ half) * COARSE_DEV + slot_c
-
+    patch_c = owner // 2
+    if n_patches == RING:
+        pairs = n_patches // 2
+        place_c = (patch_c // 2 - wide // 2 + pairs) % pairs * 2 + (patch_c ^ wide) % 2
+    else:
+        place_c = patch_c ^ wide
+    pos_c = place_c * (2 * COARSE_DEV) + (owner % 2) * COARSE_DEV + slot_c
     total = fr.shape[1] + cr.shape[1]
     spare = jnp.full((1, inc.shape[1] - total), -1, jnp.int32)
     recv_all = jnp.concatenate([recv, recv_c, spare], axis=1)
@@ -157,27 +190,14 @@
 
 
 def main_kernel(
-    n_patches, y_choices, n_pieces,
-    partner, x_rows, nl, base_f, base_c, oh2, sel, inc, shifts, nu, w_in, w_out, u_in, u_out,
+    partner, far, nl, base_f, base_c, oh2, sel, inc, shifts, nu, w_in, w_out, u_in, u_out,
     e_gain, n_gain, n_shift, *refs,
 ):
-    y_refs, refs = refs[: len(y_choices)], refs[len(y_choices) :]
-    pieces, (out, table, picks, hidden, mess) = refs[:n_pieces], refs[n_pieces:]
+    pieces, (out, table, picks, hidden, mess) = refs[:-5], refs[-5:]
+    picks[...] = jnp.concatenate([r[...] for r in pieces], axis=0)
     a = partner.shape[0]
-    b = a + x_rows.shape[0]
-    n_rows = x_rows.shape[0]
-    y_rows = y_refs[0][y_refs[0].shape[0] - n_rows :, :]
-    if len(y_choices) > 1:
-        wide, _, _, y_patch = places(n_patches)
-        pair_step = (wide // 2) ^ (y_patch // 2)
-        for k, ref in zip(y_choices[1:], y_refs[1:]):
-            y_rows = jnp.where(pair_step == k, ref[ref.shape[0] - n_rows :, :], y_rows)
-    size = picks.shape[0] // n_pieces
-    for k, r in enumerate(pieces):
-        picks[k * size : (k + 1) * size, :] = r[:size, :]
     table[0:a, :] = partner[...]
-    table[a:b, :] = x_rows[...]
-    table[b:, :] = y_rows
+    table[a:, :] = far[...]
     w_s = w_send(w_in)
     table[...] = dot(table[...], w_s).astype(BF16)
 
@@ -260,7 +280,6 @@
     )
     (pay,) = call(functools.partial(pay_kernel, halo), (nl, partner), [((2 * block, d), BF16)], limit=1)
     around = range(n_patches)
-    x_rows = lax.ppermute(pay, "wide", [(i, i ^ 1) for i in around])
     table_a = -(-2 * nodes // LANES) * LANES
     table_b = nodes + 4 * block
     padded = -(-(edges + coarse_count) // LANES) * LANES
@@ -279,24 +298,35 @@
         ],
         limit=16,
     )
+    shift = lambda v, k: lax.ppermute(v, "wide", [(i, i ^ k) for i in around])
+    x_rows = shift(pay, 1)
     known, rich = call(
         functools.partial(pair_kernel, halo), (pay, x_rows, base_c),
-        [((4 * COARSE_DEV, d), BF16), ((4 * COARSE_DEV + 2 * block, d), BF16)], limit=1,
-    )
-    shift = lambda v, k: lax.ppermute(v, "wide", [(i, i ^ k) for i in around])
-    near_ring = n_patches == 8
-    if near_ring:
-        three = shift(rich, 6)
-        two = shift(known, 4)
-        one = shift(rich, 2)
-        pieces = [known, one, two, three]
-        y_choices, y_refs = (1, 3), (one, three)
+        [((4 * COARSE_DEV, d), BF16), ((4 * COARSE_DEV + 2 * halo, d), BF16)], limit=1,
+    )
+    if n_patches == RING:
+        spot = lambda p, c: p % n_patches * 2 + c
+        split = lambda v, steps: lax.ppermute(
+            v, ("wide", "narrow"),
+            [(spot(p, c), spot(steps[c](p), c)) for p in around for c in range(2)],
+        )
+        first = split(rich, (lambda p: p + 2, lambda p: p + 4))
+        second = split(rich, (lambda p: p ^ 1, lambda p: p - 2))
+        (both,) = call(
+            both_kernel, (first, second, base_c), [((8 * COARSE_DEV + 2 * halo, d), BF16)], limit=1
+        )
+        other = lax.ppermute(both, "narrow", [(0, 1), (1, 0)])
+        far, picks = call(
+            functools.partial(collect_kernel, halo), (x_rows, known, both, other),
+            [((4 * block, d), BF16), ((16 * COARSE_DEV, d), BF16)], limit=1,
+        )
+        pieces = (picks,)
     else:
-        y_choices = (0,)
-        y_refs = (
-            lax.ppermute(
-                pay, "wide", [(i, (i - 1 if i % 2 == 0 else i + 1) % n_patches) for i in around]
-            ),
+        y_rows = lax.ppermute(
+            pay, "wide", [(i, (i - 1 if i % 2 == 0 else i + 1) % n_patches) for i in around]
+        )
+        (far,) = call(
+            functools.partial(wrap_kernel, halo), (x_rows, y_rows), [((4 * block, d), BF16)], limit=1
         )
         have = 2
         while True:
@@ -309,16 +339,16 @@
             (known,) = call(
                 join_kernel, pieces, [((len(pieces) * known.shape[0], d), BF16)], limit=2
             )
-    coarse_rows = len(pieces) * known.shape[0]
+    coarse_rows = sum(p.shape[0] for p in pieces)
 
     (base_f,) = call(
         base_kernel, (oh1, table, edge_weight_in, e_bias, fine_edges), [((edges, d), F32)], limit=16
     )
     (out,) = call(
-        functools.partial(main_kernel, n_patches, y_choices, len(pieces)),
-        (partner, x_rows, nl, base_f, base_c, oh2, sel, inc, shifts, nu,
+        main_kernel,
+        (partner, far, nl, base_f, base_c, oh2, sel, inc, shifts, nu,
          edge_weight_in, edge_weight_out, node_weight_in, node_weight_out,
-         e_gain, n_gain, n_shift, *y_refs, *pieces),
+         e_gain, n_gain, n_shift, *pieces),
         [((nodes, d), BF16)],
         scratch=[
             pltpu.VMEM((table_b, d), BF16),

time: 19.3 us -> 17.9 us (0.927)
  starting transfers between devices: 8.16 us -> 7.12 us
  waiting for transfers between devices: 4.52 us -> 4.06 us
    ppermute x3 -> x1, waiting for transfers between devices: 3.31 us -> 1.23 us  [shards(): shift = lambda v, k: lax.ppermute(v, 'wide', [(i, i ^ k) for i in around])]
    ppermute x3 -> x1, starting transfers between devices: 4.76 us -> 2.91 us  [shards(): shift = lambda v, k: lax.ppermute(v, 'wide', [(i, i ^ k) for i in around])]
    ppermute x1 -> x3, waiting for transfers between devices: 1.18 us -> 2.8 us  [the longest x2 2.79 us: shards(): lax.ppermute(v, ('wide', 'narrow'), [(spot(p, c), spot(steps[c](p), c)) f...]
    ppermute x1 -> x3, starting transfers between devices: 2.91 us -> 3.72 us  [the longest x2 3.65 us: shards(): lax.ppermute(v, ('wide', 'narrow'), [(spot(p, c), spot(steps[c](p), c)) f...]
    pallas_call x6 -> x8, Pallas kernels: 6.42 us -> 6.42 us  [call(): pl.pallas_call(kernel, out_shape=tuple((kind(*o) for o in outs)), in_spec...]
  transfers between devices with their start and end apart: 5 -> 5, of which waited for: 2 -> 2; matrix products, arithmetic and copies ran while one was open for 0% -> 0% of each run, Pallas kernels for 17% -> 18%
where the time goes in v4:
time: 17.9 us; the launch traced here: 17.7 us
  starting transfers between devices  7.12 us (40%)
  Pallas kernels  6.42 us (36%)
  waiting for transfers between devices  4.06 us (23%)
    pallas_call x8, Pallas kernels, call(): pl.pallas_call(kernel, out_shape=tuple((kind(*o) for o in outs)), in_spec...  6.42 us
    ppermute x2, starting transfers between devices, shards(): lax.ppermute(v, ('wide', 'narrow'), [(spot(p, c), spot(steps[c](p), c)) f...  3.65 us
    ppermute x1, starting transfers between devices, shards(): shift = lambda v, k: lax.ppermute(v, 'wide', [(i, i ^ k) for i in around])  2.91 us
    ppermute x2, waiting for transfers between devices, shards(): lax.ppermute(v, ('wide', 'narrow'), [(spot(p, c), spot(steps[c](p), c)) f...  2.79 us
    ppermute x1, waiting for transfers between devices, shards(): shift = lambda v, k: lax.ppermute(v, 'wide', [(i, i ^ k) for i in around])  1.23 us
    ppermute x1, starting transfers between devices, shards(): partner = lax.ppermute(node_latent, 'narrow', [(0, 1), (1, 0)])  0.49 us
  transfers between devices with their start and end apart: 5, of which 2 were waited for; matrix products, arithmetic and copies ran while one was open for 0% of the time, Pallas kernels for 18%

profile of v4, /device:TPU:0, one launch (start us, length us, event | category | flops | bytes accessed | tf_op | source)
XLA Modules:
  0.0 17.7 jit_solution(13671951932282636912)
XLA Ops:
  0.0 0.5 %collective-permute-start = (bf16[160,512]{1,0:T(8,128)(2,1)}, bf16[160,512]{1,0:T(8,128)(2,1)S(1)}, u32[]{:S(2)}, u32[]{:S(2)}) collective-permute-start(bf16[160,512]{1,0:T(8,128)(2,1)} %refs_0_.1), channel_id=1, source_target_pairs={{0,1},{1,0},{2,3},{3,2},{4,5},{5,4},{6,7},{7,6},{8,9},{9,8},{10,11... | collective-permute-start | bytes 491528 | tf_op jit(solution)/shard_map/ppermute | solution.py:276
  0.5 0.0 copy-start
  0.5 1.2 %shard_map.163 = (bf16[160,512]{1,0:T(8,128)(2,1)S(1)}, s32[1,960]{1,0:T(1,128)S(1)}, s32[1,960]{1,0:T(1,128)S(1)}, s32[1,32]{1,0:T(1,128)S(1)}, s32[1,32]{1,0:T...) custom-call(bf16[160,512]{1,0:T(8,128)(2,1)} %refs_0_.1, ...), custom_call_target="tpu_custom_call" | custom-call | tf_op jit(solution)/shard_map/pallas_call | solution.py:246
  1.7 0.0 copy-start.2
  1.7 0.0 collective-permute-done.partner
  1.8 2.9 %collective-permute-start.1 = (bf16[48,512]{1,0:T(8,128)(2,1)S(1)}, bf16[48,512]{1,0:T(8,128)(2,1)S(1)}, u32[]{:S(2)}, u32[]{:S(2)}) collective-permute-start(bf16[48,512]{1,0:T(8,128)(2,1)S(1)} %shard_map.164.pay), channel_id=1, source_target_pairs={{0,2},{2,0},{4,6},{6,4},{8,10},{10,8},{12,14},{14,12},{1,3},{3,1},... | collective-permute-start | bytes 147464 | tf_op jit(solution)/shard_map/ppermute | solution.py:301
  4.7 0.0 copy-done
  4.7 0.0 copy-done.1
  4.7 0.0 copy-done.5
  4.7 0.8 %shard_map.165 = (f32[32,512]{1,0:T(8,128)S(1)}, bf16[960,384]{1,0:T(8,128)(2,1)S(1)}, bf16[960,256]{1,0:T(8,128)(2,1)S(1)}, bf16[32,64]{1,0:T(8,128)(2,1)S(1)},...) custom-call(bf16[160,512]{1,0:T(8,128)(2,1)S(1)} %get-tuple-element., ...), custom_call_target="tpu_custom_call" | custom-call | tf_op jit(solution)/shard_map/pallas_call | solution.py:246
  5.5 1.2 %collective-permute-done.1.x_rows = bf16[48,512]{1,0:T(8,128)(2,1)S(1)} collective-permute-done((bf16[48,512]{1,0:T(8,128)(2,1)S(1)}, bf16[48,512]{1,0:T(8,128)(2,1)S(1)}, u32[]{:S(2)}, u32[]{:S(2)}) %collective-permute-start.1) | collective-permute-done | bytes 49184 | tf_op jit(solution)/shard_map/ppermute | solution.py:301
  6.7 2.2 %collective-permute-start.2 = (bf16[56,512]{1,0:T(8,128)(2,1)S(1)}, bf16[56,512]{1,0:T(8,128)(2,1)S(1)}, u32[]{:S(2)}, u32[]{:S(2)}) collective-permute-start(bf16[56,512]{1,0:T(8,128)(2,1)S(1)} %get-tuple-element.38), channel_id=1, source_target_pairs={{0,4},{1,9},{2,6},{3,11},{4,8},{5,13},{6,10},{7,15},{8,12},{9,1},{... | collective-permute-start | bytes 172040 | tf_op jit(solution)/shard_map/ppermute | solution.py:309
  8.9 1.5 %collective-permute-start.3 = (bf16[56,512]{1,0:T(8,128)(2,1)S(1)}, bf16[56,512]{1,0:T(8,128)(2,1)S(1)}, u32[]{:S(2)}, u32[]{:S(2)}) collective-permute-start(bf16[56,512]{1,0:T(8,128)(2,1)S(1)} %get-tuple-element.38), channel_id=1, source_target_pairs={{0,2},{1,13},{2,0},{3,15},{4,6},{5,1},{6,4},{7,3},{8,10},{9,5},{10... | collective-permute-start | bytes 172040 | tf_op jit(solution)/shard_map/ppermute | solution.py:309
  10.4 2.8 %collective-permute-done.2.first = bf16[56,512]{1,0:T(8,128)(2,1)S(1)} collective-permute-done((bf16[56,512]{1,0:T(8,128)(2,1)S(1)}, bf16[56,512]{1,0:T(8,128)(2,1)S(1)}, u32[]{:S(2)}, u32[]{:S(2)}) %collective-permute-start.2) | collective-permute-done | bytes 57376 | tf_op jit(solution)/shard_map/ppermute | solution.py:309
  13.2 0.0 collective-permute-done.3.second
  13.2 0.1 collective-permute-start.4
  13.3 0.0 copy-done.2
  13.3 0.0 copy-start.3
  13.3 0.0 copy-start.4
  13.3 1.2 %shard_map.169.base_f = f32[960,512]{1,0:T(8,128)S(1)} custom-call(bf16[960,384]{1,0:T(8,128)(2,1)S(1)} %get-tuple-element.40.oh1, bf16[384,512]{1,0:T(8,128)(2,1)S(1)} %get-tuple-element.41.table, bf16[1536,512]{1,0:T(8,128)(2,1)S(1)} %copy-done, f32[1,512]{1,0:T(1,128)S(1)} %get-tuple-element.33.e_bias, bf16[960,512]{1,0:T(8,128)(2,1)S(1)} %copy-done.2), custom_call_target="tpu_custom_call" | custom-call | tf_op jit(solution)/shard_map/pallas_call | solution.py:246
  14.5 0.0 collective-permute-done.4.other
  14.6 0.0 copy-done.3
  14.6 0.0 copy-done.4
  14.6 3.1 %shard_map.170 = bf16[160,512]{1,0:T(8,128)(2,1)} custom-call(bf16[160,512]{1,0:T(8,128)(2,1)S(1)} %collective-permute-done.partner, bf16[96,512]{1,0:T(8,128)(2,1)S(1)} %get-tuple-element.39.far, bf16[160,512]{1,0:T(8,128)(2,1)S(1)} %get-tuple-element.28.nl, f32[960,512]{1,0:T(8,128)S(1)} %shard_map.169.base_f, f32[32,512]{1,0:T(8,128)S(1)} %get-tuple-element.36._.base_c, ...), custom_call_target="tpu_custom_call" | custom-call | tf_op jit(solution)/shard_map/pallas_call | solution.py:246
  (6 shorter events, 0.1 us)
Async XLA Ops:
  0.0 1.7 %collective-permute-start = (bf16[160,512]{1,0:T(8,128)(2,1)}, bf16[160,512]{1,0:T(8,128)(2,1)S(1)}, u32[]{:S(2)}, u32[]{:S(2)}) collective-permute-start(bf16[160,512]{1,0:T(8,128)(2,1)} %refs_0_.1), channel_id=1, source_target_pairs={{0,1},{1,0},{2,3},{3,2},{4,5},{5,4},{6,7},{7,6},{8,9},{9,8},{10,11... | collective-permute-start | bytes 491528 | tf_op jit(solution)/shard_map/ppermute | solution.py:276
  0.5 4.2 %copy-start = (bf16[1536,512]{1,0:T(8,128)(2,1)S(1)}, bf16[1536,512]{1,0:T(8,128)(2,1)}, u32[]{:S(2)}) copy-start(bf16[1536,512]{1,0:T(8,128)(2,1)} %w_in.5) | copy-start | bytes 4718596
  0.5 4.2 %copy-start.1 = (bf16[1024,512]{1,0:T(8,128)(2,1)S(1)}, bf16[1024,512]{1,0:T(8,128)(2,1)}, u32[]{:S(2)}) copy-start(bf16[1024,512]{1,0:T(8,128)(2,1)} %u_in.3) | copy-start | bytes 3145732
  0.5 4.2 %copy-start.5 = (bf16[32,512]{1,0:T(8,128)(2,1)S(1)}, bf16[32,512]{1,0:T(8,128)(2,1)}, u32[]{:S(2)}) copy-start(bf16[32,512]{1,0:T(8,128)(2,1)} %ce.1) | copy-start | bytes 98308
  1.7 11.6 %copy-start.2 = (bf16[960,512]{1,0:T(8,128)(2,1)S(1)}, bf16[960,512]{1,0:T(8,128)(2,1)}, u32[]{:S(2)}) copy-start(bf16[960,512]{1,0:T(8,128)(2,1)} %fe.1) | copy-start | bytes 2949124
  1.8 5.0 %collective-permute-start.1 = (bf16[48,512]{1,0:T(8,128)(2,1)S(1)}, bf16[48,512]{1,0:T(8,128)(2,1)S(1)}, u32[]{:S(2)}, u32[]{:S(2)}) collective-permute-start(bf16[48,512]{1,0:T(8,128)(2,1)S(1)} %shard_map.164.pay), channel_id=1, source_target_pairs={{0,2},{2,0},{4,6},{6,4},{8,10},{10,8},{12,14},{14,12},{1,3},{3,1},... | collective-permute-start | bytes 147464 | tf_op jit(solution)/shard_map/ppermute | solution.py:301
  6.7 6.4 %collective-permute-start.2 = (bf16[56,512]{1,0:T(8,128)(2,1)S(1)}, bf16[56,512]{1,0:T(8,128)(2,1)S(1)}, u32[]{:S(2)}, u32[]{:S(2)}) collective-permute-start(bf16[56,512]{1,0:T(8,128)(2,1)S(1)} %get-tuple-element.38), channel_id=1, source_target_pairs={{0,4},{1,9},{2,6},{3,11},{4,8},{5,13},{6,10},{7,15},{8,12},{9,1},{... | collective-permute-start | bytes 172040 | tf_op jit(solution)/shard_map/ppermute | solution.py:309
  8.9 4.3 %collective-permute-start.3 = (bf16[56,512]{1,0:T(8,128)(2,1)S(1)}, bf16[56,512]{1,0:T(8,128)(2,1)S(1)}, u32[]{:S(2)}, u32[]{:S(2)}) collective-permute-start(bf16[56,512]{1,0:T(8,128)(2,1)S(1)} %get-tuple-element.38), channel_id=1, source_target_pairs={{0,2},{1,13},{2,0},{3,15},{4,6},{5,1},{6,4},{7,3},{8,10},{9,5},{10... | collective-permute-start | bytes 172040 | tf_op jit(solution)/shard_map/ppermute | solution.py:309
  13.2 1.3 %collective-permute-start.4 = (bf16[72,512]{1,0:T(8,128)(2,1)S(1)}, bf16[72,512]{1,0:T(8,128)(2,1)S(1)}, u32[]{:S(2)}, u32[]{:S(2)}) collective-permute-start(bf16[72,512]{1,0:T(8,128)(2,1)S(1)} %shard_map.167.both), channel_id=1, source_target_pairs={{0,1},{1,0},{2,3},{3,2},{4,5},{5,4},{6,7},{7,6},{8,9},{9,8},{10,11... | collective-permute-start | bytes 221192 | tf_op jit(solution)/shard_map/ppermute | solution.py:318
  13.3 1.3 %copy-start.3 = (bf16[512,512]{1,0:T(8,128)(2,1)S(1)}, bf16[512,512]{1,0:T(8,128)(2,1)}, u32[]{:S(2)}) copy-start(bf16[512,512]{1,0:T(8,128)(2,1)} %w_out.1) | copy-start | bytes 1572868
  13.3 1.3 %copy-start.4 = (bf16[512,512]{1,0:T(8,128)(2,1)S(1)}, bf16[512,512]{1,0:T(8,128)(2,1)}, u32[]{:S(2)}) copy-start(bf16[512,512]{1,0:T(8,128)(2,1)} %u_out.1) | copy-start | bytes 1572868

commit v5 on v4

--- a/solution.py
+++ b/solution.py
@@ -73,11 +73,10 @@
     rich[...] = jnp.concatenate([known[...]] + halos_of(x_rows, halo), axis=0)
 
 
-def both_kernel(first, second, _, both):
-    low = lax.axis_index("narrow") == 0
-    n, m = first.shape[0], both.shape[0] - first.shape[0]
-    both[:n, :] = jnp.where(low, first[...], second[...])
-    both[n:, :] = first[:m, :]
+def both_kernel(first, second, _, __, both):
+    n = first.shape[0]
+    both[:n, :] = first[...]
+    both[n:, :] = second[...]
 
 
 def halos_of(rows, halo):
@@ -85,19 +84,19 @@
     return [rows[:halo, :], rows[block : block + halo, :]]
 
 
-def collect_kernel(halo, x_rows, known, both, other, far, picks):
+def collect_kernel(halo, known, both, other, far, picks):
     n, m = 2 * halo, known.shape[0]
     low = lax.axis_index("narrow") == 0
     even = lax.axis_index("wide") % 2 == 0
     zero, one = jnp.where(low, both[...], other[...]), jnp.where(low, other[...], both[...])
     picks[...] = jnp.concatenate([known[...], one[:m], one[m + n :], zero[:m]], axis=0)
     source = jnp.where(even, zero[m : m + n], one[m : m + n])
-    far[...] = jnp.concatenate([x_rows[...], source, known[: 2 * COARSE_DEV]], axis=0)
-
-
-def wrap_kernel(halo, x_rows, y_rows, far):
+    far[...] = jnp.concatenate([source, known[: 2 * COARSE_DEV]], axis=0)
+
+
+def wrap_kernel(halo, y_rows, far):
     far[...] = jnp.concatenate(
-        [x_rows[...]] + halos_of(y_rows[...], halo) + [y_rows[: 2 * COARSE_DEV, :]], axis=0
+        halos_of(y_rows[...], halo) + [y_rows[: 2 * COARSE_DEV, :]], axis=0
     )
 
 
@@ -176,12 +175,9 @@
 
 
 def base_kernel(oh1, table, w_in, e_bias, fe, base_f):
-    rows, d = fe.shape
-    step = rows // 2
-    for k in range(2):
-        s = slice(k * step, (k + 1) * step)
-        own = 0.5 * (dot(fe[s, :], w_in[:d, :]) + e_bias[...])
-        base_f[s, :] = own + dot(oh1[s, :], table[...])
+    d = fe.shape[1]
+    own = 0.5 * (dot(fe[...], w_in[:d, :]) + e_bias[...])
+    base_f[...] = own + dot(oh1[...], table[...])
 
 
 def w_send(w_in):
@@ -189,17 +185,22 @@
     return w_in[d : 2 * d, :]
 
 
+def prep_kernel(partner, x_rows, w_in, ready):
+    n = partner.shape[0]
+    ready[:n, :] = dot(partner[...], w_send(w_in)).astype(BF16)
+    ready[n:, :] = dot(x_rows[...], w_send(w_in)).astype(BF16)
+
+
 def main_kernel(
-    partner, far, nl, base_f, base_c, oh2, sel, inc, shifts, nu, w_in, w_out, u_in, u_out,
+    ready, far, nl, base_f, base_c, oh2, sel, inc, shifts, nu, w_in, w_out, u_in, u_out,
     e_gain, n_gain, n_shift, *refs,
 ):
     pieces, (out, table, picks, hidden, mess) = refs[:-5], refs[-5:]
     picks[...] = jnp.concatenate([r[...] for r in pieces], axis=0)
-    a = partner.shape[0]
-    table[0:a, :] = partner[...]
-    table[a:, :] = far[...]
+    a = ready.shape[0]
     w_s = w_send(w_in)
-    table[...] = dot(table[...], w_s).astype(BF16)
+    table[:a, :] = ready[...]
+    table[a:, :] = dot(far[...], w_s).astype(BF16)
 
     rows, coarse = base_f.shape[0], base_c.shape[0]
     step = rows // CHUNKS
@@ -219,12 +220,13 @@
         mess[s, :] = normalized(dot(hidden[s, :], w_out[...])).astype(BF16)
 
     mess[rows + coarse :, :] = jnp.zeros_like(mess[rows + coarse :, :])
-    order = [CHUNKS] + list(range(CHUNKS))
-    first(order[0])
-    for now, then in zip(order, order[1:]):
-        first(then)
-        second(now)
-    second(order[-1])
+    first(CHUNKS)
+    first(0)
+    for k in range(1, CHUNKS):
+        first(k)
+        second(k - 1)
+    parts[CHUNKS - 1] = slice(parts[CHUNKS - 1].start, rows + coarse)
+    second(CHUNKS - 1)
     summed = dot(inc[...], mess[...]) * e_gain[...] + shifts[...]
     d = nl.shape[1]
     half = nu[...] + 0.5 * dot(summed.astype(BF16), u_in[d:, :])
@@ -304,21 +306,27 @@
         functools.partial(pair_kernel, halo), (pay, x_rows, base_c),
         [((4 * COARSE_DEV, d), BF16), ((4 * COARSE_DEV + 2 * halo, d), BF16)], limit=1,
     )
+    (base_f,) = call(
+        base_kernel, (oh1, table, edge_weight_in, e_bias, fine_edges), [((edges, d), F32)], limit=16
+    )
+    (ready,) = call(
+        prep_kernel, (partner, x_rows, edge_weight_in), [((nodes + 2 * block, d), BF16)], limit=4
+    )
     if n_patches == RING:
         spot = lambda p, c: p % n_patches * 2 + c
         split = lambda v, steps: lax.ppermute(
             v, ("wide", "narrow"),
             [(spot(p, c), spot(steps[c](p), c)) for p in around for c in range(2)],
         )
-        first = split(rich, (lambda p: p + 2, lambda p: p + 4))
-        second = split(rich, (lambda p: p ^ 1, lambda p: p - 2))
+        first = split(rich, (lambda p: p + 2, lambda p: p - 2))
+        second = split(known, (lambda p: p ^ 1, lambda p: p + 4))
         (both,) = call(
-            both_kernel, (first, second, base_c), [((8 * COARSE_DEV + 2 * halo, d), BF16)], limit=1
+            both_kernel, (first, second, base_f, ready), [((8 * COARSE_DEV + 2 * halo, d), BF16)], limit=1
         )
         other = lax.ppermute(both, "narrow", [(0, 1), (1, 0)])
         far, picks = call(
-            functools.partial(collect_kernel, halo), (x_rows, known, both, other),
-            [((4 * block, d), BF16), ((16 * COARSE_DEV, d), BF16)], limit=1,
+            functools.partial(collect_kernel, halo), (known, both, other),
+            [((2 * block, d), BF16), ((16 * COARSE_DEV, d), BF16)], limit=1,
         )
         pieces = (picks,)
     else:
@@ -326,7 +334,7 @@
             pay, "wide", [(i, (i - 1 if i % 2 == 0 else i + 1) % n_patches) for i in around]
         )
         (far,) = call(
-            functools.partial(wrap_kernel, halo), (x_rows, y_rows), [((4 * block, d), BF16)], limit=1
+            functools.partial(wrap_kernel, halo), (y_rows,), [((2 * block, d), BF16)], limit=1
         )
         have = 2
         while True:
@@ -341,12 +349,9 @@
             )
     coarse_rows = sum(p.shape[0] for p in pieces)
 
-    (base_f,) = call(
-        base_kernel, (oh1, table, edge_weight_in, e_bias, fine_edges), [((edges, d), F32)], limit=16
-    )
     (out,) = call(
         main_kernel,
-        (partner, far, nl, base_f, base_c, oh2, sel, inc, shifts, nu,
+        (ready, far, nl, base_f, base_c, oh2, sel, inc, shifts, nu,
          edge_weight_in, edge_weight_out, node_weight_in, node_weight_out,
          e_gain, n_gain, n_shift, *pieces),
         [((nodes, d), BF16)],

time: 17.9 us -> 17.5 us (0.978)
  waiting for transfers between devices: 4.06 us -> 3.53 us
    ppermute x2, waiting for transfers between devices: 2.79 us -> 1.18 us  [shards(): lax.ppermute(v, ('wide', 'narrow'), [(spot(p, c), spot(steps[c](p), c)) f...]
    ppermute x1, waiting for transfers between devices: 0.01 us -> 1.08 us  [shards(): other = lax.ppermute(both, 'narrow', [(0, 1), (1, 0)])]
    pallas_call x8 -> x9, Pallas kernels: 6.42 us -> 6.5 us  [call(): pl.pallas_call(kernel, out_shape=tuple((kind(*o) for o in outs)), in_spec...]
  transfers between devices with their start and end apart: 5 -> 5, of which waited for: 2 -> 4; matrix products, arithmetic and copies ran while one was open for 0% -> 0% of each run, Pallas kernels for 18% -> 20%
where the time goes in v5:
time: 17.5 us; the launch traced here: 17.4 us
  starting transfers between devices  7.23 us (41%)
  Pallas kernels  6.5 us (37%)
  waiting for transfers between devices  3.53 us (20%)
    pallas_call x9, Pallas kernels, call(): pl.pallas_call(kernel, out_shape=tuple((kind(*o) for o in outs)), in_spec...  6.5 us
    ppermute x2, starting transfers between devices, shards(): lax.ppermute(v, ('wide', 'narrow'), [(spot(p, c), spot(steps[c](p), c)) f...  3.65 us
    ppermute x1, starting transfers between devices, shards(): shift = lambda v, k: lax.ppermute(v, 'wide', [(i, i ^ k) for i in around])  2.91 us
    ppermute x1, waiting for transfers between devices, shards(): shift = lambda v, k: lax.ppermute(v, 'wide', [(i, i ^ k) for i in around])  1.24 us
    ppermute x2, waiting for transfers between devices, shards(): lax.ppermute(v, ('wide', 'narrow'), [(spot(p, c), spot(steps[c](p), c)) f...  1.18 us
    ppermute x1, waiting for transfers between devices, shards(): other = lax.ppermute(both, 'narrow', [(0, 1), (1, 0)])  1.08 us
    ppermute x1, starting transfers between devices, shards(): partner = lax.ppermute(node_latent, 'narrow', [(0, 1), (1, 0)])  0.49 us
  transfers between devices with their start and end apart: 5, of which 4 were waited for; matrix products, arithmetic and copies ran while one was open for 0% of the time, Pallas kernels for 20%

profile of v5, /device:TPU:0, one launch (start us, length us, event | category | flops | bytes accessed | tf_op | source)
XLA Modules:
  0.0 17.4 jit_solution(11705775803300057345)
XLA Ops:
  0.0 0.5 %collective-permute-start = (bf16[160,512]{1,0:T(8,128)(2,1)}, bf16[160,512]{1,0:T(8,128)(2,1)S(1)}, u32[]{:S(2)}, u32[]{:S(2)}) collective-permute-start(bf16[160,512]{1,0:T(8,128)(2,1)} %refs_0_.1), channel_id=1, source_target_pairs={{0,1},{1,0},{2,3},{3,2},{4,5},{5,4},{6,7},{7,6},{8,9},{9,8},{10,11... | collective-permute-start | bytes 491528 | tf_op jit(solution)/shard_map/ppermute | solution.py:278
  0.5 1.2 %shard_map.163 = (bf16[160,512]{1,0:T(8,128)(2,1)S(1)}, s32[1,960]{1,0:T(1,128)S(1)}, s32[1,960]{1,0:T(1,128)S(1)}, s32[1,32]{1,0:T(1,128)S(1)}, s32[1,32]{1,0:T...) custom-call(bf16[160,512]{1,0:T(8,128)(2,1)} %refs_0_.1, ...), custom_call_target="tpu_custom_call" | custom-call | tf_op jit(solution)/shard_map/pallas_call | solution.py:248
  1.7 0.0 copy-start.2
  1.7 0.0 collective-permute-done.partner
  1.8 2.9 %collective-permute-start.1 = (bf16[48,512]{1,0:T(8,128)(2,1)S(1)}, bf16[48,512]{1,0:T(8,128)(2,1)S(1)}, u32[]{:S(2)}, u32[]{:S(2)}) collective-permute-start(bf16[48,512]{1,0:T(8,128)(2,1)S(1)} %shard_map.164.pay), channel_id=1, source_target_pairs={{0,2},{2,0},{4,6},{6,4},{8,10},{10,8},{12,14},{14,12},{1,3},{3,1},... | collective-permute-start | bytes 147464 | tf_op jit(solution)/shard_map/ppermute | solution.py:303
  4.7 0.0 copy-done
  4.7 0.0 copy-done.1
  4.7 0.0 copy-done.5
  4.7 0.8 %shard_map.166 = (f32[32,512]{1,0:T(8,128)S(1)}, bf16[960,384]{1,0:T(8,128)(2,1)S(1)}, bf16[960,256]{1,0:T(8,128)(2,1)S(1)}, bf16[32,64]{1,0:T(8,128)(2,1)S(1)},...) custom-call(bf16[160,512]{1,0:T(8,128)(2,1)S(1)} %get-tuple-element., ...), custom_call_target="tpu_custom_call" | custom-call | tf_op jit(solution)/shard_map/pallas_call | solution.py:248
  5.5 1.2 %collective-permute-done.1.x_rows = bf16[48,512]{1,0:T(8,128)(2,1)S(1)} collective-permute-done((bf16[48,512]{1,0:T(8,128)(2,1)S(1)}, bf16[48,512]{1,0:T(8,128)(2,1)S(1)}, u32[]{:S(2)}, u32[]{:S(2)}) %collective-permute-start.1) | collective-permute-done | bytes 49184 | tf_op jit(solution)/shard_map/ppermute | solution.py:303
  6.7 2.2 %collective-permute-start.2 = (bf16[56,512]{1,0:T(8,128)(2,1)S(1)}, bf16[56,512]{1,0:T(8,128)(2,1)S(1)}, u32[]{:S(2)}, u32[]{:S(2)}) collective-permute-start(bf16[56,512]{1,0:T(8,128)(2,1)S(1)} %get-tuple-element.38), channel_id=1, source_target_pairs={{0,4},{1,13},{2,6},{3,15},{4,8},{5,1},{6,10},{7,3},{8,12},{9,5},{1... | collective-permute-start | bytes 172040 | tf_op jit(solution)/shard_map/ppermute | solution.py:317
  8.9 1.5 %collective-permute-start.3 = (bf16[16,512]{1,0:T(8,128)(2,1)S(1)}, bf16[16,512]{1,0:T(8,128)(2,1)S(1)}, u32[]{:S(2)}, u32[]{:S(2)}) collective-permute-start(bf16[16,512]{1,0:T(8,128)(2,1)S(1)} %get-tuple-element.37.known), channel_id=1, source_target_pairs={{0,2},{1,9},{2,0},{3,11},{4,6},{5,13},{6,4},{7,15},{8,10},{9,1},{1... | collective-permute-start | bytes 49160 | tf_op jit(solution)/shard_map/ppermute | solution.py:317
  10.4 0.0 copy-done.2
  10.4 1.2 %shard_map.168._.base_f = f32[960,512]{1,0:T(8,128)S(1)} custom-call(bf16[960,384]{1,0:T(8,128)(2,1)S(1)} %get-tuple-element.39.oh1, bf16[384,512]{1,0:T(8,128)(2,1)S(1)} %get-tuple-element.40.table, bf16[1536,512]{1,0:T(8,128)(2,1)S(1)} %copy-done, f32[1,512]{1,0:T(1,128)S(1)} %get-tuple-element.33.e_bias, bf16[960,512]{1,0:T(8,128)(2,1)S(1)} %copy-done.2), custom_call_target="tpu_custom_call" | custom-call | tf_op jit(solution)/shard_map/pallas_call | solution.py:248
  11.6 0.0 copy-start.3
  11.6 0.0 copy-start.4
  11.6 0.3 %shard_map.165.__.ready = bf16[208,512]{1,0:T(8,128)(2,1)S(1)} custom-call(bf16[160,512]{1,0:T(8,128)(2,1)S(1)} %collective-permute-done.partner, bf16[48,512]{1,0:T(8,128)(2,1)S(1)} %collective-permute-done.1.x_rows, bf16[1536,512]{1,0:T(8,128)(2,1)S(1)} %copy-done), custom_call_target="tpu_custom_call" | custom-call | tf_op jit(solution)/shard_map/pallas_call | solution.py:248
  11.9 0.7 %collective-permute-done.3.second = bf16[16,512]{1,0:T(8,128)(2,1)S(1)} collective-permute-done((bf16[16,512]{1,0:T(8,128)(2,1)S(1)}, bf16[16,512]{1,0:T(8,128)(2,1)S(1)}, u32[]{:S(2)}, u32[]{:S(2)}) %collective-permute-start.3) | collective-permute-done | bytes 16416 | tf_op jit(solution)/shard_map/ppermute | solution.py:317
  12.6 0.4 %collective-permute-done.2.first = bf16[56,512]{1,0:T(8,128)(2,1)S(1)} collective-permute-done((bf16[56,512]{1,0:T(8,128)(2,1)S(1)}, bf16[56,512]{1,0:T(8,128)(2,1)S(1)}, u32[]{:S(2)}, u32[]{:S(2)}) %collective-permute-start.2) | collective-permute-done | bytes 57376 | tf_op jit(solution)/shard_map/ppermute | solution.py:317
  13.1 0.2 %collective-permute-start.4 = (bf16[72,512]{1,0:T(8,128)(2,1)S(1)}, bf16[72,512]{1,0:T(8,128)(2,1)S(1)}, u32[]{:S(2)}, u32[]{:S(2)}) collective-permute-start(bf16[72,512]{1,0:T(8,128)(2,1)S(1)} %shard_map.169.both), channel_id=1, source_target_pairs={{0,1},{1,0},{2,3},{3,2},{4,5},{5,4},{6,7},{7,6},{8,9},{9,8},{10,11... | collective-permute-start | bytes 221192 | tf_op jit(solution)/shard_map/ppermute | solution.py:326
  13.3 1.1 %collective-permute-done.4.other = bf16[72,512]{1,0:T(8,128)(2,1)S(1)} collective-permute-done((bf16[72,512]{1,0:T(8,128)(2,1)S(1)}, bf16[72,512]{1,0:T(8,128)(2,1)S(1)}, u32[]{:S(2)}, u32[]{:S(2)}) %collective-permute-start.4) | collective-permute-done | bytes 73760 | tf_op jit(solution)/shard_map/ppermute | solution.py:326
  14.4 0.0 copy-done.3
  14.4 0.0 copy-done.4
  14.4 3.0 %shard_map.171 = bf16[160,512]{1,0:T(8,128)(2,1)} custom-call(bf16[208,512]{1,0:T(8,128)(2,1)S(1)} %shard_map.165.__.ready, bf16[48,512]{1,0:T(8,128)(2,1)S(1)} %get-tuple-element.41.far, bf16[160,512]{1,0:T(8,128)(2,1)S(1)} %get-tuple-element.28.nl, f32[960,512]{1,0:T(8,128)S(1)} %shard_map.168._.base_f, f32[32,512]{1,0:T(8,128)S(1)} %get-tuple-element.36._.base_c, ...), custom_call_target="tpu_custom_call" | custom-call | tf_op jit(solution)/shard_map/pallas_call | solution.py:248
  (7 shorter events, 0.1 us)
Async XLA Ops:
  0.0 1.7 %collective-permute-start = (bf16[160,512]{1,0:T(8,128)(2,1)}, bf16[160,512]{1,0:T(8,128)(2,1)S(1)}, u32[]{:S(2)}, u32[]{:S(2)}) collective-permute-start(bf16[160,512]{1,0:T(8,128)(2,1)} %refs_0_.1), channel_id=1, source_target_pairs={{0,1},{1,0},{2,3},{3,2},{4,5},{5,4},{6,7},{7,6},{8,9},{9,8},{10,11... | collective-permute-start | bytes 491528 | tf_op jit(solution)/shard_map/ppermute | solution.py:278
  0.5 4.2 %copy-start = (bf16[1536,512]{1,0:T(8,128)(2,1)S(1)}, bf16[1536,512]{1,0:T(8,128)(2,1)}, u32[]{:S(2)}) copy-start(bf16[1536,512]{1,0:T(8,128)(2,1)} %w_in.7) | copy-start | bytes 4718596
  0.5 4.2 %copy-start.1 = (bf16[1024,512]{1,0:T(8,128)(2,1)S(1)}, bf16[1024,512]{1,0:T(8,128)(2,1)}, u32[]{:S(2)}) copy-start(bf16[1024,512]{1,0:T(8,128)(2,1)} %u_in.3) | copy-start | bytes 3145732
  0.5 4.2 %copy-start.5 = (bf16[32,512]{1,0:T(8,128)(2,1)S(1)}, bf16[32,512]{1,0:T(8,128)(2,1)}, u32[]{:S(2)}) copy-start(bf16[32,512]{1,0:T(8,128)(2,1)} %ce.1) | copy-start | bytes 98308
  1.7 8.7 %copy-start.2 = (bf16[960,512]{1,0:T(8,128)(2,1)S(1)}, bf16[960,512]{1,0:T(8,128)(2,1)}, u32[]{:S(2)}) copy-start(bf16[960,512]{1,0:T(8,128)(2,1)} %fe.1) | copy-start | bytes 2949124
  1.8 5.0 %collective-permute-start.1 = (bf16[48,512]{1,0:T(8,128)(2,1)S(1)}, bf16[48,512]{1,0:T(8,128)(2,1)S(1)}, u32[]{:S(2)}, u32[]{:S(2)}) collective-permute-start(bf16[48,512]{1,0:T(8,128)(2,1)S(1)} %shard_map.164.pay), channel_id=1, source_target_pairs={{0,2},{2,0},{4,6},{6,4},{8,10},{10,8},{12,14},{14,12},{1,3},{3,1},... | collective-permute-start | bytes 147464 | tf_op jit(solution)/shard_map/ppermute | solution.py:303
  6.7 6.3 %collective-permute-start.2 = (bf16[56,512]{1,0:T(8,128)(2,1)S(1)}, bf16[56,512]{1,0:T(8,128)(2,1)S(1)}, u32[]{:S(2)}, u32[]{:S(2)}) collective-permute-start(bf16[56,512]{1,0:T(8,128)(2,1)S(1)} %get-tuple-element.38), channel_id=1, source_target_pairs={{0,4},{1,13},{2,6},{3,15},{4,8},{5,1},{6,10},{7,3},{8,12},{9,5},{1... | collective-permute-start | bytes 172040 | tf_op jit(solution)/shard_map/ppermute | solution.py:317
  8.9 3.7 %collective-permute-start.3 = (bf16[16,512]{1,0:T(8,128)(2,1)S(1)}, bf16[16,512]{1,0:T(8,128)(2,1)S(1)}, u32[]{:S(2)}, u32[]{:S(2)}) collective-permute-start(bf16[16,512]{1,0:T(8,128)(2,1)S(1)} %get-tuple-element.37.known), channel_id=1, source_target_pairs={{0,2},{1,9},{2,0},{3,11},{4,6},{5,13},{6,4},{7,15},{8,10},{9,1},{1... | collective-permute-start | bytes 49160 | tf_op jit(solution)/shard_map/ppermute | solution.py:317
  11.6 2.8 %copy-start.3 = (bf16[512,512]{1,0:T(8,128)(2,1)S(1)}, bf16[512,512]{1,0:T(8,128)(2,1)}, u32[]{:S(2)}) copy-start(bf16[512,512]{1,0:T(8,128)(2,1)} %w_out.1) | copy-start | bytes 1572868
  11.6 2.8 %copy-start.4 = (bf16[512,512]{1,0:T(8,128)(2,1)S(1)}, bf16[512,512]{1,0:T(8,128)(2,1)}, u32[]{:S(2)}) copy-start(bf16[512,512]{1,0:T(8,128)(2,1)} %u_out.1) | copy-start | bytes 1572868
  13.1 1.3 %collective-permute-start.4 = (bf16[72,512]{1,0:T(8,128)(2,1)S(1)}, bf16[72,512]{1,0:T(8,128)(2,1)S(1)}, u32[]{:S(2)}, u32[]{:S(2)}) collective-permute-start(bf16[72,512]{1,0:T(8,128)(2,1)S(1)} %shard_map.169.both), channel_id=1, source_target_pairs={{0,1},{1,0},{2,3},{3,2},{4,5},{5,4},{6,7},{7,6},{8,9},{9,8},{10,11... | collective-permute-start | bytes 221192 | tf_op jit(solution)/shard_map/ppermute | solution.py:326

commit v6 on v5

--- a/solution.py
+++ b/solution.py
@@ -11,6 +11,7 @@
 COARSE_DEV = 4
 LANES = 128
 CHUNKS = 3
+LATE = 128
 RING = 8
 BF16 = jnp.bfloat16
 F32 = jnp.float32
@@ -117,7 +118,7 @@
 def local_kernel(
     nodes, halo, n_patches,
     nl, fs, fr, cs, cr, e_bias, n_bias, e_shift, ce, w_in, u_in,
-    base_c, oh1, oh2, sel, inc, shifts, nu, table,
+    base_c, oh1, oh2, sel, inc_f, inc_e, inc_l, inc_c, pack, late, shifts, nu, table,
 ):
     d = nl.shape[1]
     wide, half, device, y_patch = places(n_patches)
@@ -153,13 +154,32 @@
     else:
         place_c = patch_c ^ wide
     pos_c = place_c * (2 * COARSE_DEV) + (owner % 2) * COARSE_DEV + slot_c
-    total = fr.shape[1] + cr.shape[1]
-    spare = jnp.full((1, inc.shape[1] - total), -1, jnp.int32)
-    recv_all = jnp.concatenate([recv, recv_c, spare], axis=1)
-    node_at = lax.broadcasted_iota(jnp.int32, inc.shape, 0)
-    marks = jnp.where(node_at == recv_all, 1.0, 0.0)
-    inc[...] = marks.astype(BF16)
-    shifts[...] = jnp.sum(marks, axis=1, keepdims=True) * e_shift[...]
+
+    def incidence(ids):
+        at = lax.broadcasted_iota(jnp.int32, (nodes, ids.shape[1]), 0)
+        return jnp.where(at == ids, 1.0, 0.0)
+
+    edges = fr.shape[1]
+    last_block = pos >= nodes + 2 * block
+    late_row = jnp.where(last_block, 1.0, 0.0)
+    before = lax.broadcasted_iota(jnp.int32, (edges, edges), 0)
+    before = before < lax.broadcasted_iota(jnp.int32, (edges, edges), 1)
+    flags = jnp.broadcast_to(late_row, (8, edges)).astype(BF16)
+    rank = dot(flags, jnp.where(before, 1.0, 0.0).astype(BF16))[0:1, :].astype(jnp.int32)
+    rank = jnp.where(last_block, rank, -1)
+    chosen = lax.broadcasted_iota(jnp.int32, pack.shape, 0) == rank
+    chosen = jnp.where(chosen, 1.0, 0.0).astype(BF16)
+    pack[...] = chosen
+    late[...] = late_row
+    marks, marks_c = incidence(recv), incidence(recv_c)
+    inc_f[...] = marks.astype(BF16)
+    inc_e[...] = (marks * (1.0 - late_row)).astype(BF16)
+    inc_l[...] = lax.dot_general(
+        marks.astype(BF16), chosen, (((1,), (1,)), ((), ())), preferred_element_type=F32
+    ).astype(BF16)
+    inc_c[...] = marks_c.astype(BF16)
+    count = jnp.sum(marks, axis=1, keepdims=True) + jnp.sum(marks_c, axis=1, keepdims=True)
+    shifts[...] = count * e_shift[...]
     wide_c = -(-sel.shape[1] // LANES) * LANES
     sel[...] = one_hot((columns(pos_c),), wide_c)[:, : sel.shape[1]]
     oh_c = one_hot((columns(recv_c),), table.shape[0])
@@ -174,7 +194,7 @@
     base_c[...] = 0.5 * (dot(ce[...], w_in[:d, :]) + dot(oh_c, table[...]) + e_bias[...])
 
 
-def base_kernel(oh1, table, w_in, e_bias, fe, base_f):
+def base_kernel(oh1, table, w_in, e_bias, fe, _, __, base_f):
     d = fe.shape[1]
     own = 0.5 * (dot(fe[...], w_in[:d, :]) + e_bias[...])
     base_f[...] = own + dot(oh1[...], table[...])
@@ -185,49 +205,60 @@
     return w_in[d : 2 * d, :]
 
 
-def prep_kernel(partner, x_rows, w_in, ready):
+def prep_kernel(partner, x_rows, base_f, oh2, pack, w_in, ready, hidden, late_half, late_oh):
     n = partner.shape[0]
+    m = n + x_rows.shape[0]
     ready[:n, :] = dot(partner[...], w_send(w_in)).astype(BF16)
-    ready[n:, :] = dot(x_rows[...], w_send(w_in)).astype(BF16)
-
-
-def main_kernel(
-    ready, far, nl, base_f, base_c, oh2, sel, inc, shifts, nu, w_in, w_out, u_in, u_out,
-    e_gain, n_gain, n_shift, *refs,
+    ready[n:m, :] = dot(x_rows[...], w_send(w_in)).astype(BF16)
+    ready[m:, :] = jnp.zeros_like(ready[m:, :])
+    half = base_f[...]
+    hidden[...] = silu_of_half(half + dot(oh2[...], ready[...])).astype(BF16)
+    coarse_bits = half.astype(BF16)
+    fine_bits = (half - coarse_bits.astype(F32)).astype(BF16)
+    late_half[...] = dot(pack[...], coarse_bits) + dot(pack[...], fine_bits)
+    late_oh[...] = dot(pack[...], oh2[:, oh2.shape[1] - LANES :]).astype(BF16)
+
+
+def early_kernel(hidden, inc_e, w_out, total, mess):
+    rows = hidden.shape[0]
+    step = rows // CHUNKS
+    for k in range(CHUNKS):
+        s = slice(k * step, (k + 1) * step)
+        mess[s, :] = normalized(dot(hidden[s, :], w_out[...])).astype(BF16)
+    total[...] = dot(inc_e[...], mess[...])
+
+
+def last_kernel(
+    n_pieces, ready, far, nl, base_f, base_c, oh2, sel, inc_f, inc_l, inc_c, late, late_half, late_oh,
+    total, shifts, nu, w_in, w_out, u_in, u_out, e_gain, n_gain, n_shift, *refs,
 ):
-    pieces, (out, table, picks, hidden, mess) = refs[:-5], refs[-5:]
+    pieces, (out, picks, table, hidden, mess, acc) = refs[:n_pieces], refs[n_pieces:]
+    w_s = w_send(w_in)
+    a = ready.shape[0] - far.shape[0]
+    table[:a, :] = ready[:a, :]
+    table[a:, :] = dot(far[...], w_s).astype(BF16)
     picks[...] = jnp.concatenate([r[...] for r in pieces], axis=0)
-    a = ready.shape[0]
-    w_s = w_send(w_in)
-    table[:a, :] = ready[...]
-    table[a:, :] = dot(far[...], w_s).astype(BF16)
-
-    rows, coarse = base_f.shape[0], base_c.shape[0]
-    step = rows // CHUNKS
-    parts = [slice(k * step, (k + 1) * step) for k in range(CHUNKS)] + [slice(rows, rows + coarse)]
-
-    def first(k):
-        s = parts[k]
-        if k < CHUNKS:
-            half = base_f[s, :] + dot(oh2[s, :], table[...])
-        else:
-            picked = dot(sel[...], picks[...]).astype(BF16)
-            half = base_c[...] + 0.5 * dot(picked, w_s)
-        hidden[s, :] = silu_of_half(half).astype(BF16)
-
-    def second(k):
-        s = parts[k]
-        mess[s, :] = normalized(dot(hidden[s, :], w_out[...])).astype(BF16)
-
-    mess[rows + coarse :, :] = jnp.zeros_like(mess[rows + coarse :, :])
-    first(CHUNKS)
-    first(0)
-    for k in range(1, CHUNKS):
-        first(k)
-        second(k - 1)
-    parts[CHUNKS - 1] = slice(parts[CHUNKS - 1].start, rows + coarse)
-    second(CHUNKS - 1)
-    summed = dot(inc[...], mess[...]) * e_gain[...] + shifts[...]
+    picked = dot(sel[...], picks[...]).astype(BF16)
+    n = late_half.shape[0]
+    tail = table[table.shape[0] - LANES :, :]
+    half = jnp.concatenate(
+        [late_half[...] + dot(late_oh[...], tail), base_c[...] + 0.5 * dot(picked, w_s)], axis=0
+    )
+    some = normalized(dot(silu_of_half(half).astype(BF16), w_out[...])).astype(BF16)
+    coarse_sum = dot(inc_c[...], some[n:])
+    acc[...] = total[...] + dot(inc_l[...], some[:n]) + coarse_sum
+
+    @pl.when(jnp.sum(late[...]) > n)
+    def _():
+        rows = base_f.shape[0]
+        step = rows // CHUNKS
+        for k in range(CHUNKS):
+            s = slice(k * step, (k + 1) * step)
+            hidden[s, :] = silu_of_half(base_f[s, :] + dot(oh2[s, :], table[...])).astype(BF16)
+            mess[s, :] = normalized(dot(hidden[s, :], w_out[...])).astype(BF16)
+        acc[...] = dot(inc_f[...], mess[...]) + coarse_sum
+
+    summed = acc[...] * e_gain[...] + shifts[...]
     d = nl.shape[1]
     half = nu[...] + 0.5 * dot(summed.astype(BF16), u_in[d:, :])
     update = normalized(dot(silu_of_half(half).astype(BF16), u_out[...]))
@@ -284,8 +315,7 @@
     around = range(n_patches)
     table_a = -(-2 * nodes // LANES) * LANES
     table_b = nodes + 4 * block
-    padded = -(-(edges + coarse_count) // LANES) * LANES
-    base_c, oh1, oh2, sel, inc, shifts, nu, table = call(
+    base_c, oh1, oh2, sel, inc_f, inc_e, inc_l, inc_c, pack, late, shifts, nu, table = call(
         functools.partial(local_kernel, nodes, halo, n_patches),
         (nl, fs, fr, cs, cr, e_bias, n_bias, e_shift, coarse_edges, edge_weight_in, node_weight_in),
         [
@@ -293,7 +323,12 @@
             ((edges, table_a), BF16),
             ((edges, table_b), BF16),
             ((coarse_count, 2 * n_patches * COARSE_DEV), BF16),
-            ((nodes, padded), BF16),
+            ((nodes, edges), BF16),
+            ((nodes, edges), BF16),
+            ((nodes, LATE), BF16),
+            ((nodes, coarse_count), BF16),
+            ((LATE, edges), BF16),
+            ((1, edges), F32),
             ((nodes, d), F32),
             ((nodes, d), F32),
             ((table_a, d), BF16),
@@ -307,10 +342,15 @@
         [((4 * COARSE_DEV, d), BF16), ((4 * COARSE_DEV + 2 * halo, d), BF16)], limit=1,
     )
     (base_f,) = call(
-        base_kernel, (oh1, table, edge_weight_in, e_bias, fine_edges), [((edges, d), F32)], limit=16
-    )
-    (ready,) = call(
-        prep_kernel, (partner, x_rows, edge_weight_in), [((nodes + 2 * block, d), BF16)], limit=4
+        base_kernel,
+        (oh1, table, edge_weight_in, e_bias, fine_edges, edge_weight_out, node_weight_out),
+        [((edges, d), F32)],
+        limit=16,
+    )
+    ready, hidden, late_half, late_oh = call(
+        prep_kernel, (partner, x_rows, base_f, oh2, pack, edge_weight_in),
+        [((table_b, d), BF16), ((edges, d), BF16), ((LATE, d), F32), ((LATE, LANES), BF16)],
+        limit=12,
     )
     if n_patches == RING:
         spot = lambda p, c: p % n_patches * 2 + c
@@ -349,17 +389,22 @@
             )
     coarse_rows = sum(p.shape[0] for p in pieces)
 
+    (total,) = call(
+        early_kernel, (hidden, inc_e, edge_weight_out), [((nodes, d), F32)],
+        scratch=[pltpu.VMEM((edges, d), BF16)], limit=12,
+    )
     (out,) = call(
-        main_kernel,
-        (ready, far, nl, base_f, base_c, oh2, sel, inc, shifts, nu,
-         edge_weight_in, edge_weight_out, node_weight_in, node_weight_out,
+        functools.partial(last_kernel, len(pieces)),
+        (ready, far, nl, base_f, base_c, oh2, sel, inc_f, inc_l, inc_c, late, late_half, late_oh, total,
+         shifts, nu, edge_weight_in, edge_weight_out, node_weight_in, node_weight_out,
          e_gain, n_gain, n_shift, *pieces),
         [((nodes, d), BF16)],
         scratch=[
+            pltpu.VMEM((coarse_rows, d), BF16),
             pltpu.VMEM((table_b, d), BF16),
-            pltpu.VMEM((coarse_rows, d), BF16),
-            pltpu.VMEM((padded, d), BF16),
-            pltpu.VMEM((padded, d), BF16),
+            pltpu.VMEM((edges, d), BF16),
+            pltpu.VMEM((edges, d), BF16),
+            pltpu.VMEM((nodes, d), F32),
         ],
         limit=16,
         far_out=True,

time: 17.5 us -> 16.9 us (0.966)
  waiting for transfers between devices: 3.53 us -> 1.02 us
  Pallas kernels: 6.5 us -> 8.36 us
    pallas_call x9 -> x10, Pallas kernels: 6.5 us -> 8.36 us  [call(): pl.pallas_call(kernel, out_shape=tuple((kind(*o) for o in outs)), in_spec...]
    ppermute x1, waiting for transfers between devices: 1.08 us -> 0.03 us  [shards(): other = lax.ppermute(both, 'narrow', [(0, 1), (1, 0)])]
    ppermute x2, waiting for transfers between devices: 1.18 us -> 0.18 us  [shards(): lax.ppermute(v, ('wide', 'narrow'), [(spot(p, c), spot(steps[c](p), c)) f...]
    ppermute x1, waiting for transfers between devices: 1.24 us -> 0.8 us  [shards(): shift = lambda v, k: lax.ppermute(v, 'wide', [(i, i ^ k) for i in around])]
  transfers between devices with their start and end apart: 5 -> 5, of which waited for: 4 -> 2; matrix products, arithmetic and copies ran while one was open for 0% -> 0% of each run, Pallas kernels for 20% -> 36%
where the time goes in v6:
time: 16.9 us; the launch traced here: 16.7 us
  Pallas kernels  8.36 us (49%)
  starting transfers between devices  7.23 us (43%)
  waiting for transfers between devices  1.02 us (6%)
    pallas_call x10, Pallas kernels, call(): pl.pallas_call(kernel, out_shape=tuple((kind(*o) for o in outs)), in_spec...  8.36 us
    ppermute x2, starting transfers between devices, shards(): lax.ppermute(v, ('wide', 'narrow'), [(spot(p, c), spot(steps[c](p), c)) f...  3.65 us
    ppermute x1, starting transfers between devices, shards(): shift = lambda v, k: lax.ppermute(v, 'wide', [(i, i ^ k) for i in around])  2.9 us
    ppermute x1, waiting for transfers between devices, shards(): shift = lambda v, k: lax.ppermute(v, 'wide', [(i, i ^ k) for i in around])  0.8 us
    ppermute x1, starting transfers between devices, shards(): partner = lax.ppermute(node_latent, 'narrow', [(0, 1), (1, 0)])  0.49 us
  transfers between devices with their start and end apart: 5, of which 2 were waited for; matrix products, arithmetic and copies ran while one was open for 0% of the time, Pallas kernels for 36%

profile of v6, /device:TPU:0, one launch (start us, length us, event | category | flops | bytes accessed | tf_op | source)
XLA Modules:
  0.0 16.7 jit_solution(1503050353897672231)
XLA Ops:
  0.0 0.5 %collective-permute-start = (bf16[160,512]{1,0:T(8,128)(2,1)}, bf16[160,512]{1,0:T(8,128)(2,1)S(1)}, u32[]{:S(2)}, u32[]{:S(2)}) collective-permute-start(bf16[160,512]{1,0:T(8,128)(2,1)} %refs_0_.1), channel_id=1, source_target_pairs={{0,1},{1,0},{2,3},{3,2},{4,5},{5,4},{6,7},{7,6},{8,9},{9,8},{10,11... | collective-permute-start | bytes 491528 | tf_op jit(solution)/shard_map/ppermute | solution.py:309
  0.5 1.2 %shard_map.163 = (bf16[160,512]{1,0:T(8,128)(2,1)S(1)}, s32[1,960]{1,0:T(1,128)S(1)}, s32[1,960]{1,0:T(1,128)S(1)}, s32[1,32]{1,0:T(1,128)S(1)}, s32[1,32]{1,0:T...) custom-call(bf16[160,512]{1,0:T(8,128)(2,1)} %refs_0_.1, ...), custom_call_target="tpu_custom_call" | custom-call | tf_op jit(solution)/shard_map/pallas_call | solution.py:279
  1.7 0.0 copy-start.2
  1.7 0.0 copy-start.3
  1.7 0.0 copy-start.4
  1.7 0.0 collective-permute-done.partner
  1.8 2.9 %collective-permute-start.1 = (bf16[48,512]{1,0:T(8,128)(2,1)S(1)}, bf16[48,512]{1,0:T(8,128)(2,1)S(1)}, u32[]{:S(2)}, u32[]{:S(2)}) collective-permute-start(bf16[48,512]{1,0:T(8,128)(2,1)S(1)} %shard_map.164.pay), channel_id=1, source_target_pairs={{0,2},{2,0},{4,6},{6,4},{8,10},{10,8},{12,14},{14,12},{1,3},{3,1},... | collective-permute-start | bytes 147464 | tf_op jit(solution)/shard_map/ppermute | solution.py:338
  4.7 0.0 copy-done
  4.7 0.0 copy-done.1
  4.7 0.0 copy-done.5
  4.7 1.3 %shard_map.165 = (f32[32,512]{1,0:T(8,128)S(1)}, bf16[960,384]{1,0:T(8,128)(2,1)S(1)}, bf16[960,256]{1,0:T(8,128)(2,1)S(1)}, bf16[32,64]{1,0:T(8,128)(2,1)S(1)},...) custom-call(bf16[160,512]{1,0:T(8,128)(2,1)S(1)} %get-tuple-element., ...), custom_call_target="tpu_custom_call" | custom-call | tf_op jit(solution)/shard_map/pallas_call | solution.py:279
  5.9 0.8 %collective-permute-done.1.x_rows = bf16[48,512]{1,0:T(8,128)(2,1)S(1)} collective-permute-done((bf16[48,512]{1,0:T(8,128)(2,1)S(1)}, bf16[48,512]{1,0:T(8,128)(2,1)S(1)}, u32[]{:S(2)}, u32[]{:S(2)}) %collective-permute-start.1) | collective-permute-done | bytes 49184 | tf_op jit(solution)/shard_map/ppermute | solution.py:338
  6.7 2.2 %collective-permute-start.2 = (bf16[56,512]{1,0:T(8,128)(2,1)S(1)}, bf16[56,512]{1,0:T(8,128)(2,1)S(1)}, u32[]{:S(2)}, u32[]{:S(2)}) collective-permute-start(bf16[56,512]{1,0:T(8,128)(2,1)S(1)} %get-tuple-element.52), channel_id=1, source_target_pairs={{0,4},{1,13},{2,6},{3,15},{4,8},{5,1},{6,10},{7,3},{8,12},{9,5},{1... | collective-permute-start | bytes 172040 | tf_op jit(solution)/shard_map/ppermute | solution.py:357
  8.9 1.5 %collective-permute-start.3 = (bf16[16,512]{1,0:T(8,128)(2,1)S(1)}, bf16[16,512]{1,0:T(8,128)(2,1)S(1)}, u32[]{:S(2)}, u32[]{:S(2)}) collective-permute-start(bf16[16,512]{1,0:T(8,128)(2,1)S(1)} %get-tuple-element.51.known), channel_id=1, source_target_pairs={{0,2},{1,9},{2,0},{3,11},{4,6},{5,13},{6,4},{7,15},{8,10},{9,1},{1... | collective-permute-start | bytes 49160 | tf_op jit(solution)/shard_map/ppermute | solution.py:357
  10.4 0.0 copy-done.2
  10.4 0.0 copy-done.3
  10.4 1.2 %shard_map.166.base_f._ = f32[960,512]{1,0:T(8,128)S(1)} custom-call(bf16[960,384]{1,0:T(8,128)(2,1)S(1)} %get-tuple-element.45.oh1, bf16[384,512]{1,0:T(8,128)(2,1)S(1)} %get-tuple-element.46.table, bf16[1536,512]{1,0:T(8,128)(2,1)S(1)} %copy-done, f32[1,512]{1,0:T(1,128)S(1)} %get-tuple-element.42.e_bias, bf16[960,512]{1,0:T(8,128)(2,1)S(1)} %copy-done.3, ...), custom_call_target="tpu_custom_call" | custom-call | tf_op jit(solution)/shard_map/pallas_call | solution.py:279
  11.6 1.3 %shard_map.167 = (bf16[256,512]{1,0:T(8,128)(2,1)S(1)}, bf16[960,512]{1,0:T(8,128)(2,1)S(1)}, f32[128,512]{1,0:T(8,128)S(1)}, bf16[128,128]{1,0:T(8,128)(2,1)S(1)}) custom-call(bf16[160,512]{1,0:T(8,128)(2,1)S(1)} %collective-permute-done.partner, bf16[48,512]{1,0:T(8,128)(2,1)S(1)} %collective-permute-done.1.x_rows, f32[960,512]{1,0:T(8,128)S(1)} %shard_map.166.base_f._, ...), custom_call_target="tpu_custom_call" | custom-call | tf_op jit(solution)/shard_map/pallas_call | solution.py:279
  12.9 0.0 collective-permute-done.3.second
  12.9 0.2 %collective-permute-done.2.first = bf16[56,512]{1,0:T(8,128)(2,1)S(1)} collective-permute-done((bf16[56,512]{1,0:T(8,128)(2,1)S(1)}, bf16[56,512]{1,0:T(8,128)(2,1)S(1)}, u32[]{:S(2)}, u32[]{:S(2)}) %collective-permute-start.2) | collective-permute-done | bytes 57376 | tf_op jit(solution)/shard_map/ppermute | solution.py:357
  13.1 0.2 %collective-permute-start.4 = (bf16[72,512]{1,0:T(8,128)(2,1)S(1)}, bf16[72,512]{1,0:T(8,128)(2,1)S(1)}, u32[]{:S(2)}, u32[]{:S(2)}) collective-permute-start(bf16[72,512]{1,0:T(8,128)(2,1)S(1)} %shard_map.169.both), channel_id=1, source_target_pairs={{0,1},{1,0},{2,3},{3,2},{4,5},{5,4},{6,7},{7,6},{8,9},{9,8},{10,11... | collective-permute-start | bytes 221192 | tf_op jit(solution)/shard_map/ppermute | solution.py:366
  13.3 1.0 %shard_map.171.total = f32[160,512]{1,0:T(8,128)S(1)} custom-call(bf16[960,512]{1,0:T(8,128)(2,1)S(1)} %get-tuple-element.61.hidden, bf16[160,960]{1,0:T(8,128)(2,1)S(1)} %get-tuple-element.62.inc_e, bf16[512,512]{1,0:T(8,128)(2,1)S(1)} %copy-done.2), custom_call_target="tpu_custom_call" | custom-call | tf_op jit(solution)/shard_map/pallas_call | solution.py:279
  14.3 0.0 collective-permute-done.4.other
  14.4 2.3 %shard_map.172 = bf16[160,512]{1,0:T(8,128)(2,1)} custom-call(bf16[256,512]{1,0:T(8,128)(2,1)S(1)} %get-tuple-element.49.__.ready, bf16[48,512]{1,0:T(8,128)(2,1)S(1)} %get-tuple-element.53.far, bf16[160,512]{1,0:T(8,128)(2,1)S(1)} %get-tuple-element.37.nl, f32[960,512]{1,0:T(8,128)S(1)} %shard_map.166.base_f._, f32[32,512]{1,0:T(8,128)S(1)} %get-tuple-element.50._.base_c, ...), custom_call_target="tpu_custom_call" | custom-call | tf_op jit(solution)/shard_map/pallas_call | solution.py:279
  (8 shorter events, 0.1 us)
Async XLA Ops:
  0.0 1.7 %collective-permute-start = (bf16[160,512]{1,0:T(8,128)(2,1)}, bf16[160,512]{1,0:T(8,128)(2,1)S(1)}, u32[]{:S(2)}, u32[]{:S(2)}) collective-permute-start(bf16[160,512]{1,0:T(8,128)(2,1)} %refs_0_.1), channel_id=1, source_target_pairs={{0,1},{1,0},{2,3},{3,2},{4,5},{5,4},{6,7},{7,6},{8,9},{9,8},{10,11... | collective-permute-start | bytes 491528 | tf_op jit(solution)/shard_map/ppermute | solution.py:309
  0.5 4.2 %copy-start = (bf16[1536,512]{1,0:T(8,128)(2,1)S(1)}, bf16[1536,512]{1,0:T(8,128)(2,1)}, u32[]{:S(2)}) copy-start(bf16[1536,512]{1,0:T(8,128)(2,1)} %w_in.7) | copy-start | bytes 4718596
  0.5 4.2 %copy-start.1 = (bf16[1024,512]{1,0:T(8,128)(2,1)S(1)}, bf16[1024,512]{1,0:T(8,128)(2,1)}, u32[]{:S(2)}) copy-start(bf16[1024,512]{1,0:T(8,128)(2,1)} %u_in.3) | copy-start | bytes 3145732
  0.5 4.2 %copy-start.5 = (bf16[32,512]{1,0:T(8,128)(2,1)S(1)}, bf16[32,512]{1,0:T(8,128)(2,1)}, u32[]{:S(2)}) copy-start(bf16[32,512]{1,0:T(8,128)(2,1)} %ce.1) | copy-start | bytes 98308
  1.7 8.7 %copy-start.2 = (bf16[512,512]{1,0:T(8,128)(2,1)S(1)}, bf16[512,512]{1,0:T(8,128)(2,1)}, u32[]{:S(2)}) copy-start(bf16[512,512]{1,0:T(8,128)(2,1)} %w_out.3) | copy-start | bytes 1572868
  1.7 8.7 %copy-start.3 = (bf16[960,512]{1,0:T(8,128)(2,1)S(1)}, bf16[960,512]{1,0:T(8,128)(2,1)}, u32[]{:S(2)}) copy-start(bf16[960,512]{1,0:T(8,128)(2,1)} %fe.1) | copy-start | bytes 2949124
  1.7 8.7 %copy-start.4 = (bf16[512,512]{1,0:T(8,128)(2,1)S(1)}, bf16[512,512]{1,0:T(8,128)(2,1)}, u32[]{:S(2)}) copy-start(bf16[512,512]{1,0:T(8,128)(2,1)} %u_out.1) | copy-start | bytes 1572868
  1.8 5.0 %collective-permute-start.1 = (bf16[48,512]{1,0:T(8,128)(2,1)S(1)}, bf16[48,512]{1,0:T(8,128)(2,1)S(1)}, u32[]{:S(2)}, u32[]{:S(2)}) collective-permute-start(bf16[48,512]{1,0:T(8,128)(2,1)S(1)} %shard_map.164.pay), channel_id=1, source_target_pairs={{0,2},{2,0},{4,6},{6,4},{8,10},{10,8},{12,14},{14,12},{1,3},{3,1},... | collective-permute-start | bytes 147464 | tf_op jit(solution)/shard_map/ppermute | solution.py:338
  6.7 6.3 %collective-permute-start.2 = (bf16[56,512]{1,0:T(8,128)(2,1)S(1)}, bf16[56,512]{1,0:T(8,128)(2,1)S(1)}, u32[]{:S(2)}, u32[]{:S(2)}) collective-permute-start(bf16[56,512]{1,0:T(8,128)(2,1)S(1)} %get-tuple-element.52), channel_id=1, source_target_pairs={{0,4},{1,13},{2,6},{3,15},{4,8},{5,1},{6,10},{7,3},{8,12},{9,5},{1... | collective-permute-start | bytes 172040 | tf_op jit(solution)/shard_map/ppermute | solution.py:357
  8.9 4.0 %collective-permute-start.3 = (bf16[16,512]{1,0:T(8,128)(2,1)S(1)}, bf16[16,512]{1,0:T(8,128)(2,1)S(1)}, u32[]{:S(2)}, u32[]{:S(2)}) collective-permute-start(bf16[16,512]{1,0:T(8,128)(2,1)S(1)} %get-tuple-element.51.known), channel_id=1, source_target_pairs={{0,2},{1,9},{2,0},{3,11},{4,6},{5,13},{6,4},{7,15},{8,10},{9,1},{1... | collective-permute-start | bytes 49160 | tf_op jit(solution)/shard_map/ppermute | solution.py:357
  13.1 1.3 %collective-permute-start.4 = (bf16[72,512]{1,0:T(8,128)(2,1)S(1)}, bf16[72,512]{1,0:T(8,128)(2,1)S(1)}, u32[]{:S(2)}, u32[]{:S(2)}) collective-permute-start(bf16[72,512]{1,0:T(8,128)(2,1)S(1)} %shard_map.169.both), channel_id=1, source_target_pairs={{0,1},{1,0},{2,3},{3,2},{4,5},{5,4},{6,7},{7,6},{8,9},{9,8},{10,11... | collective-permute-start | bytes 221192 | tf_op jit(solution)/shard_map/ppermute | solution.py:366
